TPU v7x, 32 devices: a whole 2x2x4 slice. The times are simulated.
32 devices in a mesh: ctx: 8 (over z, x), head: 4 (over y, core).
Axes of the slice: x: 2, y: 2, z: 4, core: 2. Of those that a mesh axis runs over, the one named last changes fastest.
Arguments:
- keys: bfloat16 [16384, 5120], P('ctx', 'head'), may hold values from -6 to 6
- values: bfloat16 [16384, 5120], P('ctx', 'head'), may hold values from -6 to 6
- queries: bfloat16 [16384, 5120], P('ctx', 'head'), may hold values from -6 to 6
- rates: float32 [16384, 16], P('ctx', 'head'), may hold values from 9.765625e-05 to 0.0009765625
- w_gate: bfloat16 [320, 16, 320], P('ctx', 'head'), may hold values from -0.3125 to 0.3125
- w_up: bfloat16 [320, 16, 320], P('ctx', 'head'), may hold values from -0.3125 to 0.3125
- w_down: bfloat16 [320, 16, 320], P('ctx', 'head'), may hold values from -0.3125 to 0.3125
- gain: float32 [5120], P('head'), may hold values from 0.5 to 1.5
Outputs:
- output: bfloat16 [16384, 5120], P('ctx', 'head')
- new_gate: bfloat16 [320, 16, 320], P('ctx', 'head')
- new_up: bfloat16 [320, 16, 320], P('ctx', 'head')
- new_down: bfloat16 [320, 16, 320], P('ctx', 'head')
All inputs are finite; a program needn't handle non-finite values.
Results may differ from a plain program's by a relative error of at most 0.0092.
Values may be sent and summed in bfloat16 or wider, within the bound.
A program may use at most 128 MiB of HBM per device.

v0:
```python
import functools
import math

import jax
import jax.numpy as jnp
from jax import lax
from jax.experimental import pallas as pl
from jax.experimental.pallas import tpu as pltpu
from jax.sharding import PartitionSpec as P

EPS = 1e-06


def inner_size(n):
    inner = 1
    while inner * inner * 4 <= n and n % (inner * 2) == 0:
        inner *= 2
    return inner if inner > 1 or n % 2 else 2


def place(n, inner):
    me = lax.axis_index("ctx")
    return me, me // inner, lax.rem(me, inner), n // inner


def greet(z, x, outer, inner):
    barrier = pltpu.get_barrier_semaphore()
    for s in range(1, outer):
        pl.semaphore_signal(barrier, inc=1, device_id={"ctx": lax.rem(z + s, outer) * inner + x})
    for t in range(1, inner):
        pl.semaphore_signal(barrier, inc=1, device_id={"ctx": z * inner + lax.rem(x + t, inner)})
    pl.semaphore_wait(barrier, outer + inner - 2)


def spread(z, x, outer, inner, own_ref, out_ref, send_sem, recv_sem):
    me = z * inner + x
    copies = {}

    def send(src, block, device, s, t):
        copy = pltpu.make_async_remote_copy(
            src_ref=src,
            dst_ref=out_ref.at[block],
            send_sem=send_sem.at[s, t],
            recv_sem=recv_sem.at[s, t],
            device_id={"ctx": device},
        )
        copy.start()
        copies[s, t] = copy

    for s in range(1, outer):
        send(own_ref, me, lax.rem(z + s, outer) * inner + x, s, 0)
    for t in range(1, inner):
        send(own_ref, me, z * inner + lax.rem(x + t, inner), 0, t)
    for s in range(1, outer):
        copies[s, 0].wait_recv()
        block = lax.rem(z + outer - s, outer) * inner + x
        for t in range(1, inner):
            send(out_ref.at[block], block, z * inner + lax.rem(x + t, inner), s, t)
    for (s, t), copy in copies.items():
        if t:
            copy.wait_recv()
    for copy in copies.values():
        copy.wait_send()


def gather_kernel(n, inner, own_ref, out_ref, local_sem, send_sem, recv_sem):
    me, z, x, outer = place(n, inner)
    greet(z, x, outer, inner)
    keep = pltpu.make_async_copy(own_ref, out_ref.at[me], local_sem)
    keep.start()
    spread(z, x, outer, inner, own_ref, out_ref, send_sem, recv_sem)
    keep.wait()


def update_kernel(
    n, inner, grad_ref, old_ref, out_ref, near, part, far, fresh,
    local_sem, near_send, near_recv, far_send, far_recv, send_sem, recv_sem,
):
    me, z, x, outer = place(n, inner)
    greet(z, x, outer, inner)
    order = list(range(1, outer)) + [0]
    first = {}
    for s in order:
        row = lax.rem(z + s, outer) * inner
        for t in range(1, inner):
            column = lax.rem(x + t, inner)
            copy = pltpu.make_async_remote_copy(
                src_ref=grad_ref.at[row + column],
                dst_ref=near.at[s, t - 1],
                send_sem=near_send.at[s, t],
                recv_sem=near_recv.at[s, t],
                device_id={"ctx": z * inner + column},
            )
            copy.start()
            first[s, t] = copy
    second = {}
    total = None
    for s in order:
        row = lax.rem(z + s, outer) * inner
        total = grad_ref[row + x].astype(jnp.float32)
        for t in range(1, inner):
            first[s, t].wait_recv()
            total = total + near[s, t - 1].astype(jnp.float32)
        if s:
            part[s] = total.astype(part.dtype)
            copy = pltpu.make_async_remote_copy(
                src_ref=part.at[s],
                dst_ref=far.at[s],
                send_sem=far_send.at[s],
                recv_sem=far_recv.at[s],
                device_id={"ctx": row + x},
            )
            copy.start()
            second[s] = copy
    for s, copy in second.items():
        copy.wait_recv()
        total = total + far[s].astype(jnp.float32)
    old = old_ref[...].astype(jnp.float32)
    updated = old + total
    old_sq = jnp.sum(old * old, axis=1, keepdims=True)
    new_sq = jnp.sum(updated * updated, axis=1, keepdims=True)
    fresh[...] = (updated * (jnp.sqrt(old_sq) * lax.rsqrt(new_sq + EPS))).astype(fresh.dtype)
    keep = pltpu.make_async_copy(fresh, out_ref.at[me], local_sem)
    keep.start()
    keep.wait()
    spread(z, x, outer, inner, out_ref.at[me], out_ref, send_sem, recv_sem)
    for copy in first.values():
        copy.wait_send()
    for copy in second.values():
        copy.wait_send()


def vmem(count):
    return [pl.BlockSpec(memory_space=pltpu.VMEM)] * count


def gather(own, n):
    inner = inner_size(n)
    outer = n // inner
    return pl.pallas_call(
        functools.partial(gather_kernel, n, inner),
        out_shape=jax.ShapeDtypeStruct((n,) + own.shape, own.dtype),
        in_specs=vmem(1),
        out_specs=vmem(1)[0],
        scratch_shapes=[pltpu.SemaphoreType.DMA]
        + [pltpu.SemaphoreType.DMA((outer, inner))] * 2,
        compiler_params=pltpu.CompilerParams(collective_id=0, has_side_effects=True),
        name="gather_weights",
    )(own)


def update(grads, old, n):
    inner = inner_size(n)
    outer = n // inner
    block = grads.shape[1:]
    return pl.pallas_call(
        functools.partial(update_kernel, n, inner),
        out_shape=jax.ShapeDtypeStruct(grads.shape, grads.dtype),
        in_specs=vmem(2),
        out_specs=vmem(1)[0],
        scratch_shapes=[
            pltpu.VMEM((outer, max(inner - 1, 1)) + block, grads.dtype),
            pltpu.VMEM((outer,) + block, grads.dtype),
            pltpu.VMEM((outer,) + block, grads.dtype),
            pltpu.VMEM(block, grads.dtype),
            pltpu.SemaphoreType.DMA,
        ]
        + [pltpu.SemaphoreType.DMA((outer, inner))] * 2
        + [pltpu.SemaphoreType.DMA((outer,))] * 2
        + [pltpu.SemaphoreType.DMA((outer, inner))] * 2,
        compiler_params=pltpu.CompilerParams(collective_id=1, has_side_effects=True),
        name="update_weights",
    )(grads, old)


def dot(a, b, left, right):
    return lax.dot_general(a, b, (((left,), (right,)), ((), ())), preferred_element_type=jnp.float32)


def grads_kernel(key_ref, value_ref, rate_ref, weight_ref, out_ref, acc):
    step = pl.program_id(0)

    @pl.when(step == 0)
    def _():
        acc[...] = jnp.zeros_like(acc)

    heads, width = weight_ref.shape[1:3]
    for h in range(heads):
        columns = slice(h * width, (h + 1) * width)
        key = key_ref[:, columns]
        gpre = dot(key, weight_ref[0, h], 1, 0)
        upre = dot(key, weight_ref[1, h], 1, 0)
        scaled = (value_ref[:, columns].astype(jnp.float32) * rate_ref[:, h : h + 1]).astype(jnp.bfloat16)
        back = dot(scaled, weight_ref[2, h], 1, 0)
        sig = jax.nn.sigmoid(gpre)
        act = gpre * sig
        slope = sig * (1.0 + gpre * (1.0 - sig))
        acc[0, h] += dot(key, (back * upre * slope).astype(jnp.bfloat16), 0, 0)
        acc[1, h] += dot(key, (back * act).astype(jnp.bfloat16), 0, 0)
        acc[2, h] += dot(scaled, (act * upre).astype(jnp.bfloat16), 0, 0)

    @pl.when(step == pl.num_programs(0) - 1)
    def _():
        out_ref[...] = acc[...].astype(out_ref.dtype)


def apply_kernel(query_ref, weight_ref, out_ref, square_ref):
    heads, width = weight_ref.shape[1:3]
    squares = None
    for h in range(heads):
        columns = slice(h * width, (h + 1) * width)
        query = query_ref[:, columns]
        gate = dot(query, weight_ref[0, h], 1, 0)
        up = dot(query, weight_ref[1, h], 1, 0)
        mixed = (jax.nn.silu(gate) * up).astype(jnp.bfloat16)
        out = dot(mixed, weight_ref[2, h], 1, 1)
        part = jnp.sum(out * out, axis=1, keepdims=True)
        squares = part if squares is None else squares + part
        out_ref[:, columns] = out.astype(out_ref.dtype)
    square_ref[...] = squares


def tile(rows, width):
    return pl.BlockSpec((rows, width), lambda i: (i, 0))


def fixed(shape):
    return pl.BlockSpec(shape, lambda i: (0,) * len(shape))


def token_grads(keys, values, rates, weights):
    rows, width = keys.shape
    step = math.gcd(rows, 512)
    return pl.pallas_call(
        grads_kernel,
        grid=(rows // step,),
        out_shape=jax.ShapeDtypeStruct(weights.shape, jnp.bfloat16),
        in_specs=[tile(step, width), tile(step, width), tile(step, rates.shape[1]), fixed(weights.shape)],
        out_specs=fixed(weights.shape),
        scratch_shapes=[pltpu.VMEM(weights.shape, jnp.float32)],
        name="token_grads",
    )(keys, values, rates, weights)


def apply(queries, weights):
    rows, width = queries.shape
    step = math.gcd(rows, 512)
    return pl.pallas_call(
        apply_kernel,
        grid=(rows // step,),
        out_shape=(
            jax.ShapeDtypeStruct((rows, width), jnp.bfloat16),
            jax.ShapeDtypeStruct((rows, 1), jnp.float32),
        ),
        in_specs=[tile(step, width), fixed(weights.shape)],
        out_specs=(tile(step, width), tile(step, 1)),
        name="apply_weights",
    )(queries, weights)


def per_device(n, width_all, keys, values, queries, rates, w_gate, w_up, w_down, gain):
    rows = keys.shape[0]
    units, heads, width = w_gate.shape
    f32 = jnp.float32
    own = jnp.stack([w_gate, w_up, w_down]).transpose(0, 2, 1, 3)
    own = own.reshape(3 * heads, units, width)
    full = gather(own, n).transpose(1, 3, 0, 2)
    full = full.reshape(3, heads, width, n * units)
    grads = token_grads(keys, values, rates, full)
    block = (n, 3 * heads * width // n, n * units)
    old = lax.dynamic_index_in_dim(full.reshape(block), lax.axis_index("ctx"), 0, keepdims=False)
    fresh = update(grads.reshape(block), old, n).reshape(full.shape)
    mine = lax.dynamic_slice_in_dim(fresh, lax.axis_index("ctx") * units, units, 3)
    mine = mine.transpose(0, 3, 1, 2)
    outs, squares = apply(queries, fresh)
    squares = lax.psum(squares.reshape(rows), "head")
    scale = lax.rsqrt(squares / width_all + EPS)
    output = (outs.astype(f32) * scale[:, None] * gain[None]).astype(jnp.bfloat16)
    return (output, mine[0], mine[1], mine[2])


def solution(mesh):
    weight = P("ctx", "head", None)
    token = P("ctx", "head")

    def whole(keys, *rest):
        body = functools.partial(per_device, mesh.shape["ctx"], keys.shape[1])
        return jax.shard_map(
            body,
            mesh=mesh,
            in_specs=(token,) * 4 + (weight,) * 3 + (P("head"),),
            out_specs=(token, weight, weight, weight),
            check_vma=False,
        )(keys, *rest)

    return whole
```

profile of v0, /device:TPU:22, one launch (start us, length us, event | category | flops | bytes accessed | tf_op | source)
XLA Modules:
  0.0 240.0 jit_solution(17123676697850397283)
XLA Ops:
  0.6 1.3 maximum_bitcast_fusion
  2.0 0.8 copy.18
  2.8 2.1 copy.20.rate_ref
  4.9 46.4 %gather_weights.1 = bf16[8,12,40,320]{3,2,1,0:T(8,128)(2,1)} custom-call(bf16[12,40,320]{2,1,0:T(8,128)(2,1)} %bitcast.27), custom_call_target="tpu_custom_call" | custom-call | tf_op jit(solution)/shard_map/gather_weights/pallas_call | solution.py:140
  51.3 2.3 copy.19
  53.6 2.9 %copy.21.weight_ref = bf16[3,4,320,320]{3,2,1,0:T(8,128)(2,1)} copy(bf16[3,4,320,320]{2,3,1,0:T(8,128)(2,1)S(1)} %bitcast.26) | data formatting | bytes 4915200 | tf_op jit(solution)/shard_map/reshape | solution.py:268
  56.5 0.0 copy-start
  56.5 28.9 %token_grads.1 = bf16[3,4,320,320]{3,2,1,0:T(8,128)(2,1)} custom-call(bf16[2048,1280]{1,0:T(8,128)(2,1)} %key_ref.1, bf16[2048,1280]{1,0:T(8,128)(2,1)} %value_ref.1, f32[2048,4]{1,0:T(8,128)} %copy.20.rate_ref, bf16[3,4,320,320]{3,2,1,0:T(8,128)(2,1)} %copy.21.weight_ref), custom_call_target="tpu_custom_call" | custom-call | tf_op jit(solution)/shard_map/token_grads/pallas_call | solution.py:234
  85.4 0.0 copy-done
  85.4 2.5 %copy.22 = bf16[12,320,8,40]{1,0,3,2:T(8,128)(2,1)} copy(bf16[12,320,8,40]{1,3,0,2:T(8,128)(2,1)S(1)} %bitcast.22) | data formatting | bytes 4915200 | tf_op jit(solution)/shard_map/transpose | solution.py:267
  87.9 6.3 %reshape_reshape.3 = bf16[8,480,320]{1,0,2:T(8,128)(2,1)S(1)} reshape(bf16[12,320,8,40]{1,0,3,2:T(8,128)(2,1)} %copy.22) | data formatting | bytes 4915200 | tf_op jit(solution)/shard_map/reshape;reshape | solution.py:271
  94.3 0.7 constant_dynamic-slice_fusion
  95.0 1.3 copy.23
  96.2 106.2 %update_weights.1 = bf16[8,480,320]{2,1,0:T(8,128)(2,1)} custom-call(bf16[8,480,320]{2,1,0:T(8,128)(2,1)} %bitcast.25, bf16[480,320]{1,0:T(8,128)(2,1)} %bitcast.28), custom_call_target="tpu_custom_call" | custom-call | tf_op jit(solution)/shard_map/update_weights/pallas_call | solution.py:156
  202.4 1.9 dynamic-slice_bitcast_fusion
  204.4 0.1 slice_bitcast_fusion
  204.4 0.0 copy-start.1
  204.5 0.8 copy.26
  205.3 0.8 copy.25
  206.1 0.8 copy.24
  206.9 19.4 %apply_weights.1 = (bf16[2048,1280]{1,0:T(8,128)(2,1)}, f32[2048,1]{1,0:T(8,128)}) custom-call(bf16[2048,1280]{1,0:T(8,128)(2,1)} %query_ref.1, bf16[3,4,320,320]{3,2,1,0:T(8,128)(2,1)} %bitcast.24), custom_call_target="tpu_custom_call" | custom-call | tf_op jit(solution)/shard_map/apply_weights/pallas_call | solution.py:248
  226.3 1.6 reduce
  227.9 6.0 %psum.7 = f32[2048]{0:T(1024)S(1)} all-reduce(f32[2048]{0:T(1024)S(1)} %reduce), channel_id=1, replica_groups=mesh['ctx'=8,'head'=4] {'head'}, use_global_device_ids=true, to_apply=%region_0.1 | all-reduce | flops 2048 | bytes 16384 | tf_op jit(solution)/shard_map/psum | solution.py:276
  233.9 0.0 copy-done.1
  233.9 6.1 %multiply_convert_fusion = bf16[2048,1280]{1,0:T(8,128)(2,1)} fusion(bf16[2048,1280]{1,0:T(8,128)(2,1)} %get-tuple-element.6, f32[1280]{0:T(1024)S(1)} %copy-done.1, f32[2048]{0:T(1024)S(1)} %add_rsqrt_fusion), kind=kLoop, calls=%fused_computation | loop fusion | flops 10485760 | bytes 10499072 | tf_op jit(solution)/shard_map/convert_element_type | solution.py:278
  (1 shorter events, 0.0 us)
Async XLA Ops:
  56.5 28.9 %copy-start = (bf16[8,12,40,320]{3,2,1,0:T(8,128)(2,1)S(1)}, bf16[8,12,40,320]{3,2,1,0:T(8,128)(2,1)}, u32[]{:S(2)}) copy-start(bf16[8,12,40,320]{3,2,1,0:T(8,128)(2,1)} %gather_weights.1) | copy-start | bytes 7372804
  204.4 29.4 %copy-start.1 = (f32[1280]{0:T(1024)S(1)}, f32[1280]{0:T(1024)}, u32[]{:S(2)}) copy-start(f32[1280]{0:T(1024)} %param.15) | copy-start | bytes 15364
where the time goes:
time: 241 us; the launch traced here: 240 us
  Pallas kernels  201 us (83%)
  local copies, waits for them, and re-layouts  23.4 us (10%)
  other arithmetic  9 us (4%)
  blocking collectives  5.98 us (2%)
    pallas_call x1, Pallas kernels, update(): pl.pallas_call(functools.partial(update_kernel, n, inner), out_shape=jax....  106 us
    pallas_call x1, Pallas kernels, gather(): pl.pallas_call(functools.partial(gather_kernel, n, inner), out_shape=jax....  46.4 us
    pallas_call x1, Pallas kernels, token_grads(): pl.pallas_call(grads_kernel, grid=(rows // step,), out_shape=jax.ShapeDty...  28.9 us
    pallas_call x1, Pallas kernels, apply(): pl.pallas_call(apply_kernel, grid=(rows // step,), out_shape=(jax.ShapeDt...  19.4 us
    another operation x1, local copies, waits for them, and re-layouts, per_device(): full.reshape(block)  6.33 us
    convert_element_type x1, other arithmetic, per_device(): (outs.astype(f32) * scale[:, None] * gain[None]).astype(jnp.bfloat16)  6.1 us
    psum x1, blocking collectives, per_device(): squares = lax.psum(squares.reshape(rows), 'head')  5.98 us
    transpose x2, local copies, waits for them, and re-layouts, per_device(): full = gather(own, n).transpose(1, 3, 0, 2)  4.83 us

commit v1 on v0

--- a/solution.py
+++ b/solution.py
@@ -258,10 +258,452 @@
     )(queries, weights)
 
 
-def per_device(n, width_all, keys, values, queries, rates, w_gate, w_up, w_down, gain):
+def fits(n, rows, units, heads, width):
+    inner = inner_size(n)
+    return (
+        inner == 2
+        and n // inner >= 2
+        and units % 8 == 0
+        and heads % 2 == 0
+        and heads <= 8
+        and width % 128 == 64
+        and rows % 512 == 0
+        and rows * heads * width <= 2048 * 1280
+    )
+
+
+class Plan:
+    def __init__(self, n, peers, rows, units, heads, width, width_all):
+        self.n, self.peers, self.rows, self.units = n, peers, rows, units
+        self.heads, self.width, self.width_all = heads, width, width_all
+        self.inner = 2
+        self.outer = n // 2
+        self.step = 512
+        self.window = width + 64
+        self.packed = 2 * width + self.window
+        self.starts = (0, width - 64, 2 * width)
+        self.shifts = (0, 64, 0)
+
+    def columns(self, h):
+        start = (h // 2) * 2 * self.width + (h % 2) * (self.width - 64)
+        return slice(start, start + self.window)
+
+    def move(self, x, old, new):
+        size = x.shape[1]
+        if old != new:
+            x = pltpu.roll(x, (new - old) % size, 1)
+        lane = lax.broadcasted_iota(jnp.int32, x.shape, 1)
+        return jnp.where((lane >= new) & (lane < new + self.width), x, 0.0)
+
+    def pack(self, gate, up, down):
+        first = self.width - 64
+        shared = gate[:, first:] + up[:, :128]
+        return jnp.concatenate([gate[:, :first], shared, up[:, 128:], down], axis=1)
+
+
+def fused_kernel(
+    plan, key_hbm, value_hbm, query_hbm, rate_ref, gate_ref, up_ref, down_ref, gain_ref,
+    out_hbm, fresh_ref,
+    keys, values, queries, rate, old, new, own, ups, downs, side, updated, weights, acc,
+    squares_old, outs, squares, row, rows_in,
+    load_sem, store_sem,
+    line_send, line_recv, cross_send, cross_recv,
+    part_send, part_recv, side_send, side_recv, row_send, row_recv,
+):
+    f32, b16 = jnp.float32, jnp.bfloat16
+    n, outer, heads, units, width = plan.n, plan.outer, plan.heads, plan.units, plan.width
+    window, step, tokens = plan.window, plan.step, plan.rows
+    me = lax.axis_index("ctx")
+    z, x = me // 2, lax.rem(me, 2)
+    mine = lax.axis_index("head")
+    other = z * 2 + 1 - x
+
+    loads = []
+    half = 2 * width
+    for p in range(heads // 2):
+        cut = slice(p * half, (p + 1) * half)
+        for i, (src, dst) in enumerate(((key_hbm, keys), (value_hbm, values), (query_hbm, queries))):
+            copy = pltpu.make_async_copy(src.at[:, cut], dst.at[:, cut], load_sem.at[i, p])
+            if i < 2:
+                copy.start()
+            loads.append((i, p, copy))
+    for i, p, copy in loads:
+        if i == 2:
+            copy.start()
+
+    barrier = pltpu.get_barrier_semaphore()
+    pl.semaphore_signal(barrier, inc=1, device_id={"ctx": other})
+    for t in range(1, plan.peers):
+        pl.semaphore_signal(barrier, inc=1, device_id={"head": lax.rem(mine + t, plan.peers)})
+
+    hops = sorted({1, outer - 1})
+    for t in hops:
+        pl.semaphore_signal(barrier, inc=1, device_id={"ctx": lax.rem(z + t, outer) * 2 + x})
+
+    for h in range(heads):
+        parts = []
+        for j, ref in enumerate((gate_ref, up_ref, down_ref)):
+            piece = ref[:, h, :].astype(f32)
+            piece = jnp.concatenate([piece, jnp.zeros((units, 64), f32)], axis=1)
+            parts.append(plan.move(piece, 0, plan.shifts[j]))
+        old[h, me] = plan.pack(*parts).astype(b16)
+
+    pl.semaphore_wait(barrier, plan.peers + len(hops))
+
+    sends = []
+
+    def send(when, make):
+        def start():
+            make().start()
+
+        def finish():
+            make().wait_send()
+
+        if when is None:
+            start()
+            sends.append(finish)
+        else:
+            pl.when(when)(start)
+            sends.append(lambda: pl.when(when)(finish))
+
+    def line_copy(g, h, origin, up):
+        buf = (old, new)[g]
+        block = origin * 2 + x
+        return pltpu.make_async_remote_copy(
+            src_ref=buf.at[h, block], dst_ref=buf.at[h, block],
+            send_sem=line_send.at[g, h, up, origin], recv_sem=line_recv.at[g, h, origin],
+            device_id={"ctx": me + (2 if up else -2)},
+        )
+
+    def cross_copy(g, h, origin):
+        buf = (old, new)[g]
+        block = origin * 2 + x
+        return pltpu.make_async_remote_copy(
+            src_ref=buf.at[h, block], dst_ref=buf.at[h, block],
+            send_sem=cross_send.at[g, h, origin], recv_sem=cross_recv.at[g, h, origin],
+            device_id={"ctx": other},
+        )
+
+    def issue(g, h):
+        send(z < outer - 1, lambda: line_copy(g, h, z, 1))
+        send(z > 0, lambda: line_copy(g, h, z, 0))
+        send(None, lambda: cross_copy(g, h, z))
+
+    def relay(g, h, d):
+        low, high = z - d, z + d
+
+        @pl.when(low >= 0)
+        def _():
+            line_copy(g, h, low, 1).wait_recv()
+
+        send((low >= 0) & (z < outer - 1), lambda: line_copy(g, h, low, 1))
+        send(low >= 0, lambda: cross_copy(g, h, low))
+
+        @pl.when(high < outer)
+        def _():
+            line_copy(g, h, high, 0).wait_recv()
+
+        send((high < outer) & (z > 0), lambda: line_copy(g, h, high, 0))
+        send(high < outer, lambda: cross_copy(g, h, high))
+
+    def arrived(g, h):
+        for o in range(outer):
+            cross_copy(g, h, o).wait_recv()
+
+    def part_copy(h, up, to):
+        buf = (downs, ups)[up]
+        return pltpu.make_async_remote_copy(
+            src_ref=own.at[h, pl.ds(to * 2, 2)], dst_ref=buf.at[h, to],
+            send_sem=part_send.at[h, up, to], recv_sem=part_recv.at[h, up, to],
+            device_id={"ctx": me + (2 if up else -2)},
+        )
+
+    def add_part(h, up, to):
+        buf = (downs, ups)[up]
+        part_copy(h, up, to).wait_recv()
+        total = own[h, pl.ds(to * 2, 2)].astype(f32) + buf[h, to].astype(f32)
+        own[h, pl.ds(to * 2, 2)] = total.astype(b16)
+
+    def reduce_start(h):
+        for to in range(outer - 1, 0, -1):
+            send(z == 0, functools.partial(part_copy, h, 1, to))
+            send(z == outer - 1, functools.partial(part_copy, h, 0, outer - 1 - to))
+
+    def reduce_relay(h, to):
+        back = outer - 1 - to
+
+        @pl.when((z > 0) & (z < to))
+        def _():
+            add_part(h, 1, to)
+
+        send((z > 0) & (z < to), lambda: part_copy(h, 1, to))
+
+        @pl.when((z < outer - 1) & (z > back))
+        def _():
+            add_part(h, 0, back)
+
+        send((z < outer - 1) & (z > back), lambda: part_copy(h, 0, back))
+
+    def side_copy(h):
+        return pltpu.make_async_remote_copy(
+            src_ref=own.at[h, other], dst_ref=side.at[h],
+            send_sem=side_send.at[h], recv_sem=side_recv.at[h],
+            device_id={"ctx": other},
+        )
+
+    def reduce_side(h):
+        @pl.when(z > 0)
+        def _():
+            add_part(h, 1, z)
+
+        @pl.when(z < outer - 1)
+        def _():
+            add_part(h, 0, z)
+
+        send(None, lambda: side_copy(h))
+
+    def reduce_end(h):
+        side_copy(h).wait_recv()
+        total = own[h, me].astype(f32) + side[h].astype(f32) + old[h, me].astype(f32)
+        updated[h] = total
+        new[h, me] = total.astype(b16)
+        issue(1, h)
+
+    def pieces(g, h, j):
+        buf = (old, new)[g]
+        start, shift = plan.starts[j], plan.shifts[j]
+        for b in range(n):
+            piece = buf[h, b, :, start : start + window].astype(f32)
+            yield b, plan.move(piece, shift, 64 * (h % 2))
+
+    def prepare_old(h):
+        for j in range(3):
+            total = jnp.zeros((1, window), f32)
+            for b, piece in pieces(0, h, j):
+                weights[j, b * units : (b + 1) * units] = piece.astype(b16)
+                total = total + jnp.sum(piece * piece, axis=0, keepdims=True)
+            squares_old[3 * h + j : 3 * h + j + 1, :] = total
+
+    def prepare_new(h):
+        for j in range(3):
+            total = jnp.zeros((1, window), f32)
+            for b, piece in pieces(1, h, j):
+                total = total + jnp.sum(piece * piece, axis=0, keepdims=True)
+            scale = jnp.sqrt(squares_old[3 * h + j : 3 * h + j + 1, :]) * lax.rsqrt(total + EPS)
+            for b, piece in pieces(1, h, j):
+                weights[j, b * units : (b + 1) * units] = (piece * scale).astype(b16)
+            start, shift = plan.starts[j], plan.shifts[j]
+            exact = plan.move(updated[h, :, start : start + window], shift, 64 * (h % 2)) * scale
+            fresh_ref[j, h] = plan.move(exact, 64 * (h % 2), 0)[:, :width].astype(b16)
+
+    def at_steps(i, slots):
+        for k, events in slots.items():
+            if events:
+                def run(events=events):
+                    for event in events:
+                        event()
+                pl.when(i == k)(run)
+
+    def grads(h, slots):
+        for j in range(3):
+            acc[j] = jnp.zeros(acc.shape[1:], f32)
+        cut = plan.columns(h)
+
+        for k in range(tokens // step):
+            for event in slots.get(k, ()):
+                event()
+
+        def body(i, _):
+            span = pl.ds(pl.multiple_of(i * step, step), step)
+            key = keys[span, cut]
+            scaled = (values[span, cut].astype(f32) * rate[span, h : h + 1]).astype(b16)
+            gpre = dot(weights[0], key, 1, 1)
+            upre = dot(weights[1], key, 1, 1)
+            back = dot(weights[2], scaled, 1, 1)
+            sig = jax.nn.sigmoid(gpre)
+            act = gpre * sig
+            slope = sig * (1.0 + gpre * (1.0 - sig))
+            acc[0] += dot((back * upre * slope).astype(b16), key, 1, 0)
+            acc[1] += dot((back * act).astype(b16), key, 1, 0)
+            acc[2] += dot((act * upre).astype(b16), scaled, 1, 0)
+            return 0
+
+        lax.fori_loop(0, tokens // step, body, 0)
+        shift = 64 * (h % 2)
+        for b in range(n):
+            parts = [
+                plan.move(acc[j, b * units : (b + 1) * units], shift, plan.shifts[j]) for j in range(3)
+            ]
+            own[h, b] = plan.pack(*parts).astype(b16)
+        reduce_start(h)
+
+    def apply_head(h):
+        cut = plan.columns(h)
+
+        def body(i, _):
+            span = pl.ds(pl.multiple_of(i * step, step), step)
+            query = queries[span, cut]
+            gate = dot(query, weights[0], 1, 1)
+            up = dot(query, weights[1], 1, 1)
+            mixed = (jax.nn.silu(gate) * up).astype(b16)
+            out = dot(mixed, weights[2], 1, 0)
+            if h % 2:
+                shared = slice(cut.start, cut.start + 128)
+                outs[span, shared] = outs[span, shared] + out[:, :128]
+                outs[span, cut.start + 128 : cut.stop] = out[:, 128:]
+            else:
+                outs[span, cut] = out
+            part = out * out
+            total = part[:, :128]
+            for c in range(128, window, 128):
+                total = total + part[:, c : c + 128]
+            squares[span, :] = total if h == 0 else squares[span, :] + total
+            return 0
+
+        lax.fori_loop(0, tokens // step, body, 0)
+
+    issue(0, 0)
+    if heads > 1:
+        issue(0, 1)
+    turned = jnp.concatenate([rate_ref[...], jnp.zeros((8 - heads, tokens), f32)], axis=0) if heads < 8 else rate_ref[...]
+    rate[...] = turned.T
+    for h in range(heads):
+        for d in range(1, outer):
+            relay(0, h, d)
+        if h + 2 < heads:
+            issue(0, h + 2)
+    for h in range(heads):
+        if h % 2 == 0:
+            for i, p, copy in loads:
+                if p == h // 2 and i < 2:
+                    copy.wait()
+        arrived(0, h)
+        prepare_old(h)
+        grads(h, {})
+        if h > 0:
+            for to in range(outer - 1, 0, -1):
+                reduce_relay(h - 1, to)
+            reduce_side(h - 1)
+    for to in range(outer - 1, 0, -1):
+        reduce_relay(heads - 1, to)
+    reduce_side(heads - 1)
+    for h in range(heads):
+        reduce_end(h)
+        for d in range(1, outer):
+            relay(1, h, d)
+    for h in range(heads):
+        if h % 2 == 0:
+            for i, p, copy in loads:
+                if p == h // 2 and i == 2:
+                    copy.wait()
+        arrived(1, h)
+        prepare_new(h)
+        apply_head(h)
+
+    row[...] = jnp.sum(squares[...].T, axis=0, keepdims=True)
+
+    def row_copy(t):
+        return pltpu.make_async_remote_copy(
+            src_ref=row, dst_ref=rows_in.at[t - 1],
+            send_sem=row_send.at[t - 1], recv_sem=row_recv.at[t - 1],
+            device_id={"head": lax.rem(mine + t, plan.peers)},
+        )
+
+    for t in range(1, plan.peers):
+        send(None, functools.partial(row_copy, t))
+    total = row[...]
+    for t in range(1, plan.peers):
+        row_copy(t).wait_recv()
+        total = total + rows_in[t - 1]
+    row_scale = lax.rsqrt(total / plan.width_all + EPS)
+    column = jnp.broadcast_to(row_scale, (128, tokens)).T
+    squares[...] = column
+
+    def finish(i):
+        span = pl.ds(pl.multiple_of(i * step, step), step)
+        return pltpu.make_async_copy(keys.at[span], out_hbm.at[span], store_sem.at[i])
+
+    def body(i, _):
+        span = pl.ds(pl.multiple_of(i * step, step), step)
+        for c in range(0, heads * width, 128):
+            scaled = outs[span, c : c + 128] * squares[span, :] * gain_ref[:, c : c + 128]
+            keys[span, c : c + 128] = scaled.astype(b16)
+        finish(i).start()
+        return 0
+
+    lax.fori_loop(0, tokens // step, body, 0)
+    for done in sends:
+        done()
+    for i in range(tokens // step):
+        finish(i).wait()
+
+
+def fused(n, peers, width_all, keys, values, queries, rates, w_gate, w_up, w_down, gain):
+    rows = keys.shape[0]
+    units, heads, width = w_gate.shape
+    plan = Plan(n, peers, rows, units, heads, width, width_all)
+    f32, b16 = jnp.float32, jnp.bfloat16
+    outer = plan.outer
+    hbm = pl.BlockSpec(memory_space=pl.ANY)
+    block = (units, plan.packed)
+    dma = pltpu.SemaphoreType.DMA
+    return pl.pallas_call(
+        functools.partial(fused_kernel, plan),
+        out_shape=(
+            jax.ShapeDtypeStruct(keys.shape, b16),
+            jax.ShapeDtypeStruct((3, heads, units, width), b16),
+        ),
+        in_specs=[hbm] * 3 + vmem(5),
+        out_specs=(hbm, vmem(1)[0]),
+        scratch_shapes=[
+            pltpu.VMEM(keys.shape, b16),
+            pltpu.VMEM(keys.shape, b16),
+            pltpu.VMEM(keys.shape, b16),
+            pltpu.VMEM((rows, 8), f32),
+            pltpu.VMEM((heads, n) + block, b16),
+            pltpu.VMEM((heads, n) + block, b16),
+            pltpu.VMEM((heads, n) + block, b16),
+            pltpu.VMEM((heads, outer, 2) + block, b16),
+            pltpu.VMEM((heads, outer, 2) + block, b16),
+            pltpu.VMEM((heads,) + block, b16),
+            pltpu.VMEM((heads,) + block, f32),
+            pltpu.VMEM((3, n * units, plan.window), b16),
+            pltpu.VMEM((3, n * units, plan.window), f32),
+            pltpu.VMEM((3 * heads, plan.window), f32),
+            pltpu.VMEM(keys.shape, f32),
+            pltpu.VMEM((rows, 128), f32),
+            pltpu.VMEM((1, rows), f32),
+            pltpu.VMEM((peers - 1, 1, rows), f32),
+            dma((3, heads // 2)),
+            dma((rows // plan.step,)),
+            dma((2, heads, 2, outer)),
+            dma((2, heads, outer)),
+            dma((2, heads, outer)),
+            dma((2, heads, outer)),
+            dma((heads, 2, outer)),
+            dma((heads, 2, outer)),
+            dma((heads,)),
+            dma((heads,)),
+            dma((peers - 1,)),
+            dma((peers - 1,)),
+        ],
+        compiler_params=pltpu.CompilerParams(
+            collective_id=2, has_side_effects=True, vmem_limit_bytes=67043328
+        ),
+        name="fused_layer",
+    )(keys, values, queries, rates.T, w_gate, w_up, w_down, gain[None])
+
+
+def per_device(n, peers, width_all, keys, values, queries, rates, w_gate, w_up, w_down, gain):
     rows = keys.shape[0]
     units, heads, width = w_gate.shape
     f32 = jnp.float32
+    if fits(n, rows, units, heads, width):
+        output, fresh = fused(
+            n, peers, width_all, keys, values, queries, rates, w_gate, w_up, w_down, gain
+        )
+        fresh = fresh.transpose(0, 2, 1, 3)
+        return (output, fresh[0], fresh[1], fresh[2])
     own = jnp.stack([w_gate, w_up, w_down]).transpose(0, 2, 1, 3)
     own = own.reshape(3 * heads, units, width)
     full = gather(own, n).transpose(1, 3, 0, 2)
@@ -284,7 +726,9 @@
     token = P("ctx", "head")
 
     def whole(keys, *rest):
-        body = functools.partial(per_device, mesh.shape["ctx"], keys.shape[1])
+        body = functools.partial(
+            per_device, mesh.shape["ctx"], mesh.shape["head"], keys.shape[1]
+        )
         return jax.shard_map(
             body,
             mesh=mesh,

time: 241 us -> 185 us (0.77)
  the two profiles are of different devices: /device:TPU:22 before, /device:TPU:0 now
where the time goes in v1:
time: 185 us
  Pallas kernels  175 us (95%)
  local copies, waits for them, and re-layouts  9.62 us (5%)
    pallas_call x1, Pallas kernels, fused(): pl.pallas_call(functools.partial(fused_kernel, plan), out_shape=(jax.Shap...  175 us
    unnamed x4, local copies, waits for them, and re-layouts  7.27 us

profile of v1, /device:TPU:0, one launch (start us, length us, event | category | flops | bytes accessed | tf_op | source)
XLA Modules:
  0.0 184.8 jit_solution(6397563835143147919)
XLA Ops:
  0.6 1.3 broadcast_in_dim.3.gain_ref
  1.9 174.5 %fused_layer.1 = (bf16[2048,1280]{1,0:T(8,128)(2,1)}, bf16[3,4,40,320]{3,2,1,0:T(8,128)(2,1)}) custom-call(bf16[2048,1280]{1,0:T(8,128)(2,1)} %key_hbm.1, bf16[2048,1280]{1,0:T(8,128)(2,1)} %value_hbm.1, bf16[2048,1280]{1,0:T(8,128)(2,1)} %query_hbm.1, f32[4,2048]{1,0:T(4,128)} %bitcast.9, bf16[40,4,320]{2,1,0:T(4,128)(2,1)} %gate_ref.1, ...), custom_call_target="tpu_custom_call" | custom-call | tf_op jit(solution)/shard_map/fused_layer/pallas_call | solution.py:650
  176.4 1.1 slice_bitcast_fusion
  177.5 0.7 copy.14
  178.2 0.7 copy.13
  178.9 0.7 copy.12
  179.6 5.2 %copy.16 = bf16[2048,1280]{1,0:T(8,128)(2,1)} copy(bf16[2048,1280]{1,0:T(8,128)(2,1)} %get-tuple-element.19) | data formatting | bytes 10485760

commit v2 on v1

--- a/solution.py
+++ b/solution.py
@@ -9,6 +9,37 @@
 from jax.sharding import PartitionSpec as P
 
 EPS = 1e-06
+
+ISSUE, RELAY, CROSS, READY, STEP, START, SIDE, PART, END, FINISH = range(10)
+ORDERS = {
+    (4, 4, 4): (
+        (0, 1, 1, 1),
+        ((0, 0, 0, 0), (0, 1, 0, 1)),
+        (
+            (ISSUE, 0, 0), (ISSUE, 0, 1), (RELAY, 0, 0, 1), (RELAY, 0, 1, 1), (RELAY, 0, 0, 2),
+            (RELAY, 0, 1, 2), (RELAY, 0, 0, 3), (ISSUE, 0, 2), (RELAY, 0, 1, 3), (ISSUE, 0, 3),
+            (RELAY, 0, 2, 1), (READY, 0, 0), (STEP, 0, 0, 0), (STEP, 0, 0, 1), (RELAY, 0, 2, 2),
+            (STEP, 0, 0, 2), (RELAY, 0, 3, 1), (STEP, 0, 0, 3), (RELAY, 0, 2, 3), (START, 0),
+            (READY, 0, 1), (STEP, 0, 1, 0), (RELAY, 0, 3, 2), (STEP, 0, 1, 1), (STEP, 0, 1, 2),
+            (RELAY, 0, 3, 3), (STEP, 0, 1, 3), (PART, 0, 3, 1), (START, 1), (READY, 0, 2),
+            (STEP, 0, 2, 0), (STEP, 0, 2, 1), (STEP, 0, 2, 2), (PART, 0, 2, 1), (PART, 0, 3, 2),
+            (STEP, 0, 2, 3), (SIDE, 1, 0), (START, 2), (SIDE, 1, 3), (READY, 0, 3), (SIDE, 1, 2),
+            (STEP, 0, 3, 0), (SIDE, 1, 1), (STEP, 0, 3, 1), (PART, 1, 3, 1), (STEP, 0, 3, 2),
+            (SIDE, 2, 3), (PART, 1, 2, 1), (END, 0), (SIDE, 2, 0), (STEP, 0, 3, 3),
+            (PART, 1, 3, 2), (PART, 2, 3, 1), (START, 3), (SIDE, 2, 2), (FINISH, 0), (SIDE, 2, 1),
+            (END, 1), (FINISH, 1), (SIDE, 3, 3), (PART, 2, 3, 2), (RELAY, 1, 0, 1),
+            (PART, 2, 2, 1), (SIDE, 3, 0), (SIDE, 3, 2), (RELAY, 1, 0, 2), (RELAY, 1, 1, 1),
+            (PART, 3, 3, 1), (SIDE, 3, 1), (END, 2), (RELAY, 1, 0, 3), (RELAY, 1, 1, 2),
+            (FINISH, 2), (PART, 3, 2, 1), (PART, 3, 3, 2), (RELAY, 1, 1, 3), (CROSS, 1, 1),
+            (RELAY, 1, 2, 1), (END, 3), (READY, 1, 0), (FINISH, 3), (STEP, 1, 0, 0),
+            (STEP, 1, 0, 1), (STEP, 1, 0, 2), (RELAY, 1, 2, 2), (STEP, 1, 0, 3), (READY, 1, 1),
+            (RELAY, 1, 3, 1), (STEP, 1, 1, 0), (RELAY, 1, 2, 3), (STEP, 1, 1, 1), (STEP, 1, 1, 2),
+            (RELAY, 1, 3, 2), (STEP, 1, 1, 3), (CROSS, 1, 3), (READY, 1, 2), (RELAY, 1, 3, 3),
+            (STEP, 1, 2, 0), (STEP, 1, 2, 1), (STEP, 1, 2, 2), (STEP, 1, 2, 3), (READY, 1, 3),
+            (STEP, 1, 3, 0), (STEP, 1, 3, 1), (STEP, 1, 3, 2), (STEP, 1, 3, 3),
+        ),
+    ),
+}
 
 
 def inner_size(n):
@@ -269,6 +300,7 @@
         and width % 128 == 64
         and rows % 512 == 0
         and rows * heads * width <= 2048 * 1280
+        and (n // inner, heads, rows // 512) in ORDERS
     )
 
 
@@ -307,7 +339,7 @@
     keys, values, queries, rate, old, new, own, ups, downs, side, updated, weights, acc,
     squares_old, outs, squares, row, rows_in,
     load_sem, store_sem,
-    line_send, line_recv, cross_send, cross_recv,
+    line_send, line_recv, cross_send, cross_recv, pass_send, pass_recv,
     part_send, part_recv, side_send, side_recv, row_send, row_recv,
 ):
     f32, b16 = jnp.float32, jnp.bfloat16
@@ -351,6 +383,7 @@
     pl.semaphore_wait(barrier, plan.peers + len(hops))
 
     sends = []
+    side_first, passing, order = ORDERS[outer, heads, tokens // step]
 
     def send(when, make):
         def start():
@@ -363,8 +396,8 @@
             start()
             sends.append(finish)
         else:
-            pl.when(when)(start)
-            sends.append(lambda: pl.when(when)(finish))
+            pl.when(when())(start)
+            sends.append(lambda: pl.when(when())(finish))
 
     def line_copy(g, h, origin, up):
         buf = (old, new)[g]
@@ -385,35 +418,57 @@
         )
 
     def issue(g, h):
-        send(z < outer - 1, lambda: line_copy(g, h, z, 1))
-        send(z > 0, lambda: line_copy(g, h, z, 0))
+        send(lambda: z < outer - 1, lambda: line_copy(g, h, z, 1))
+        send(lambda: z > 0, lambda: line_copy(g, h, z, 0))
         send(None, lambda: cross_copy(g, h, z))
 
     def relay(g, h, d):
-        low, high = z - d, z + d
-
-        @pl.when(low >= 0)
+        whole = d > 1 or not passing[g][h]
+
+        @pl.when(z >= d)
         def _():
-            line_copy(g, h, low, 1).wait_recv()
-
-        send((low >= 0) & (z < outer - 1), lambda: line_copy(g, h, low, 1))
-        send(low >= 0, lambda: cross_copy(g, h, low))
-
-        @pl.when(high < outer)
+            line_copy(g, h, z - d, 1).wait_recv()
+
+        send(lambda: (z >= d) & (z < outer - 1), lambda: line_copy(g, h, z - d, 1))
+        if whole:
+            send(lambda: z >= d, lambda: cross_copy(g, h, z - d))
+
+        @pl.when(z + d < outer)
         def _():
-            line_copy(g, h, high, 0).wait_recv()
-
-        send((high < outer) & (z > 0), lambda: line_copy(g, h, high, 0))
-        send(high < outer, lambda: cross_copy(g, h, high))
+            line_copy(g, h, z + d, 0).wait_recv()
+
+        send(lambda: (z + d < outer) & (z > 0), lambda: line_copy(g, h, z + d, 0))
+        if whole:
+            send(lambda: z + d < outer, lambda: cross_copy(g, h, z + d))
+
+    def pass_copy(g, h, up):
+        buf = (old, new)[g]
+        return pltpu.make_async_remote_copy(
+            src_ref=buf.at[h, other], dst_ref=buf.at[h, other],
+            send_sem=pass_send.at[g, h, up], recv_sem=pass_recv.at[g, h, up],
+            device_id={"ctx": me + (2 if up else -2)},
+        )
+
+    def cross(g, h):
+        cross_copy(g, h, z).wait_recv()
+        send(lambda: z < outer - 1, lambda: pass_copy(g, h, 1))
+        send(lambda: z > 0, lambda: pass_copy(g, h, 0))
 
     def arrived(g, h):
+        if not passing[g][h]:
+            for o in range(outer):
+                cross_copy(g, h, o).wait_recv()
+            return
         for o in range(outer):
-            cross_copy(g, h, o).wait_recv()
+            pl.when((o > z + 1) | (o < z - 1))(lambda: cross_copy(g, h, o).wait_recv())
+        pl.when(z > 0)(lambda: pass_copy(g, h, 1).wait_recv())
+        pl.when(z < outer - 1)(lambda: pass_copy(g, h, 0).wait_recv())
 
     def part_copy(h, up, to):
         buf = (downs, ups)[up]
+        first, count = (to * 2 + x, 1) if side_first[h] else (to * 2, 2)
         return pltpu.make_async_remote_copy(
-            src_ref=own.at[h, pl.ds(to * 2, 2)], dst_ref=buf.at[h, to],
+            src_ref=own.at[h, pl.ds(first, count)], dst_ref=buf.at[h, to, pl.ds(0, count)],
             send_sem=part_send.at[h, up, to], recv_sem=part_recv.at[h, up, to],
             device_id={"ctx": me + (2 if up else -2)},
         )
@@ -421,37 +476,52 @@
     def add_part(h, up, to):
         buf = (downs, ups)[up]
         part_copy(h, up, to).wait_recv()
-        total = own[h, pl.ds(to * 2, 2)].astype(f32) + buf[h, to].astype(f32)
-        own[h, pl.ds(to * 2, 2)] = total.astype(b16)
+        for c in range(1 if side_first[h] else 2):
+            block = to * 2 + (x if side_first[h] else c)
+            total = own[h, block].astype(f32) + buf[h, to, c].astype(f32)
+            own[h, block] = total.astype(b16)
+
+    def side_copy(h, to):
+        return pltpu.make_async_remote_copy(
+            src_ref=own.at[h, to * 2 + 1 - x], dst_ref=side.at[h, to if side_first[h] else 0],
+            send_sem=side_send.at[h, to], recv_sem=side_recv.at[h, to],
+            device_id={"ctx": other},
+        )
 
     def reduce_start(h):
+        if side_first[h]:
+            for i in range(outer):
+                send(None, functools.partial(side_copy, h, i // 2 if i % 2 else outer - 1 - i // 2))
+            return
         for to in range(outer - 1, 0, -1):
-            send(z == 0, functools.partial(part_copy, h, 1, to))
-            send(z == outer - 1, functools.partial(part_copy, h, 0, outer - 1 - to))
-
-    def reduce_relay(h, to):
+            send(lambda: z == 0, functools.partial(part_copy, h, 1, to))
+            send(lambda: z == outer - 1, functools.partial(part_copy, h, 0, outer - 1 - to))
+
+    def reduce_beside(h, to):
+        side_copy(h, to).wait_recv()
+        total = own[h, to * 2 + x].astype(f32) + side[h, to].astype(f32)
+        own[h, to * 2 + x] = total.astype(b16)
+        if to > 0:
+            send(lambda: z == 0, lambda: part_copy(h, 1, to))
+        if to < outer - 1:
+            send(lambda: z == outer - 1, lambda: part_copy(h, 0, to))
+
+    def reduce_relay(h, to, d):
         back = outer - 1 - to
 
-        @pl.when((z > 0) & (z < to))
+        @pl.when(z == d)
         def _():
             add_part(h, 1, to)
 
-        send((z > 0) & (z < to), lambda: part_copy(h, 1, to))
-
-        @pl.when((z < outer - 1) & (z > back))
+        send(lambda: z == d, lambda: part_copy(h, 1, to))
+
+        @pl.when(z == outer - 1 - d)
         def _():
             add_part(h, 0, back)
 
-        send((z < outer - 1) & (z > back), lambda: part_copy(h, 0, back))
-
-    def side_copy(h):
-        return pltpu.make_async_remote_copy(
-            src_ref=own.at[h, other], dst_ref=side.at[h],
-            send_sem=side_send.at[h], recv_sem=side_recv.at[h],
-            device_id={"ctx": other},
-        )
-
-    def reduce_side(h):
+        send(lambda: z == outer - 1 - d, lambda: part_copy(h, 0, back))
+
+    def reduce_end(h):
         @pl.when(z > 0)
         def _():
             add_part(h, 1, z)
@@ -460,11 +530,14 @@
         def _():
             add_part(h, 0, z)
 
-        send(None, lambda: side_copy(h))
-
-    def reduce_end(h):
-        side_copy(h).wait_recv()
-        total = own[h, me].astype(f32) + side[h].astype(f32) + old[h, me].astype(f32)
+        if not side_first[h]:
+            send(None, lambda: side_copy(h, z))
+
+    def renew(h):
+        total = own[h, me].astype(f32) + old[h, me].astype(f32)
+        if not side_first[h]:
+            side_copy(h, z).wait_recv()
+            total = total + side[h, 0].astype(f32)
         updated[h] = total
         new[h, me] = total.astype(b16)
         issue(1, h)
@@ -497,23 +570,19 @@
             fresh_ref[j, h] = plan.move(exact, 64 * (h % 2), 0)[:, :width].astype(b16)
 
     def at_steps(i, slots):
-        for k, events in slots.items():
-            if events:
-                def run(events=events):
-                    for event in events:
-                        event()
-                pl.when(i == k)(run)
+        for k, events in sorted(slots.items()):
+            @pl.when(i == k)
+            def _():
+                for event in events:
+                    event()
 
     def grads(h, slots):
         for j in range(3):
             acc[j] = jnp.zeros(acc.shape[1:], f32)
         cut = plan.columns(h)
 
-        for k in range(tokens // step):
-            for event in slots.get(k, ()):
-                event()
-
         def body(i, _):
+            at_steps(i, slots)
             span = pl.ds(pl.multiple_of(i * step, step), step)
             key = keys[span, cut]
             scaled = (values[span, cut].astype(f32) * rate[span, h : h + 1]).astype(b16)
@@ -529,6 +598,8 @@
             return 0
 
         lax.fori_loop(0, tokens // step, body, 0)
+
+    def start(h):
         shift = 64 * (h % 2)
         for b in range(n):
             parts = [
@@ -537,10 +608,11 @@
             own[h, b] = plan.pack(*parts).astype(b16)
         reduce_start(h)
 
-    def apply_head(h):
+    def apply_head(h, slots):
         cut = plan.columns(h)
 
         def body(i, _):
+            at_steps(i, slots)
             span = pl.ds(pl.multiple_of(i * step, step), step)
             query = queries[span, cut]
             gate = dot(query, weights[0], 1, 1)
@@ -562,43 +634,40 @@
 
         lax.fori_loop(0, tokens // step, body, 0)
 
-    issue(0, 0)
-    if heads > 1:
-        issue(0, 1)
-    turned = jnp.concatenate([rate_ref[...], jnp.zeros((8 - heads, tokens), f32)], axis=0) if heads < 8 else rate_ref[...]
-    rate[...] = turned.T
-    for h in range(heads):
-        for d in range(1, outer):
-            relay(0, h, d)
-        if h + 2 < heads:
-            issue(0, h + 2)
-    for h in range(heads):
+    def loaded(h, kinds):
         if h % 2 == 0:
             for i, p, copy in loads:
-                if p == h // 2 and i < 2:
+                if p == h // 2 and i in kinds:
                     copy.wait()
-        arrived(0, h)
-        prepare_old(h)
-        grads(h, {})
-        if h > 0:
-            for to in range(outer - 1, 0, -1):
-                reduce_relay(h - 1, to)
-            reduce_side(h - 1)
-    for to in range(outer - 1, 0, -1):
-        reduce_relay(heads - 1, to)
-    reduce_side(heads - 1)
-    for h in range(heads):
-        reduce_end(h)
-        for d in range(1, outer):
-            relay(1, h, d)
-    for h in range(heads):
-        if h % 2 == 0:
-            for i, p, copy in loads:
-                if p == h // 2 and i == 2:
-                    copy.wait()
-        arrived(1, h)
-        prepare_new(h)
-        apply_head(h)
+
+    def ready(g, h):
+        loaded(h, (2,) if g else (0, 1))
+        arrived(g, h)
+        (prepare_new if g else prepare_old)(h)
+
+    handlers = {
+        ISSUE: issue, RELAY: relay, CROSS: cross, READY: ready, START: start, SIDE: reduce_beside,
+        PART: reduce_relay, END: reduce_end, FINISH: renew,
+    }
+    turned = rate_ref[...]
+    if heads < 8:
+        turned = jnp.concatenate([turned, jnp.zeros((8 - heads, tokens), f32)], axis=0)
+    rate[...] = turned.T
+
+    order = list(order)
+    while order:
+        event = order.pop(0)
+        if event[0] != READY:
+            handlers[event[0]](*event[1:])
+            continue
+        ready(*event[1:])
+        slots = {}
+        for k in range(tokens // step):
+            while order[0][0] != STEP:
+                kind, *rest = order.pop(0)
+                slots.setdefault(k, []).append(functools.partial(handlers[kind], *rest))
+            order.pop(0)
+        (apply_head if event[1] else grads)(event[2], slots)
 
     row[...] = jnp.sum(squares[...].T, axis=0, keepdims=True)
 
@@ -665,7 +734,7 @@
             pltpu.VMEM((heads, n) + block, b16),
             pltpu.VMEM((heads, outer, 2) + block, b16),
             pltpu.VMEM((heads, outer, 2) + block, b16),
-            pltpu.VMEM((heads,) + block, b16),
+            pltpu.VMEM((heads, outer) + block, b16),
             pltpu.VMEM((heads,) + block, f32),
             pltpu.VMEM((3, n * units, plan.window), b16),
             pltpu.VMEM((3, n * units, plan.window), f32),
@@ -680,10 +749,12 @@
             dma((2, heads, outer)),
             dma((2, heads, outer)),
             dma((2, heads, outer)),
+            dma((2, heads, 2)),
+            dma((2, heads, 2)),
             dma((heads, 2, outer)),
             dma((heads, 2, outer)),
-            dma((heads,)),
-            dma((heads,)),
+            dma((heads, outer)),
+            dma((heads, outer)),
             dma((peers - 1,)),
             dma((peers - 1,)),
         ],

time: 185 us -> 114 us (0.62)
  Pallas kernels: 175 us -> 104 us
    pallas_call x1, Pallas kernels: 175 us -> 104 us  [fused(): pl.pallas_call(functools.partial(fused_kernel, plan), out_shape=(jax.Shap...]
where the time goes in v2:
time: 114 us
  Pallas kernels  104 us (91%)
  local copies, waits for them, and re-layouts  9.62 us (8%)
    pallas_call x1, Pallas kernels, fused(): pl.pallas_call(functools.partial(fused_kernel, plan), out_shape=(jax.Shap...  104 us
    unnamed x4, local copies, waits for them, and re-layouts  7.27 us

profile of v2, /device:TPU:0, one launch (start us, length us, event | category | flops | bytes accessed | tf_op | source)
XLA Modules:
  0.0 113.8 jit_solution(14408551059246564634)
XLA Ops:
  0.6 1.3 %broadcast_in_dim.3.gain_ref = f32[1,1280]{1,0:T(1,128)} reshape(f32[1280]{0:T(1024)} %param.15) | data formatting | bytes 10240 | tf_op jit(solution)/shard_map/broadcast_in_dim | solution.py:765
  1.9 103.5 %fused_layer.1 = (bf16[2048,1280]{1,0:T(8,128)(2,1)}, bf16[3,4,40,320]{3,2,1,0:T(8,128)(2,1)}) custom-call(bf16[2048,1280]{1,0:T(8,128)(2,1)} %key_hbm.1, bf16[2048,1280]{1,0:T(8,128)(2,1)} %value_hbm.1, bf16[2048,1280]{1,0:T(8,128)(2,1)} %query_hbm.1, f32[4,2048]{1,0:T(4,128)} %bitcast.9, bf16[40,4,320]{2,1,0:T(4,128)(2,1)} %gate_ref.1, ...), custom_call_target="tpu_custom_call" | custom-call | tf_op jit(solution)/shard_map/fused_layer/pallas_call | solution.py:719
  105.5 1.1 slice_bitcast_fusion
  106.5 0.7 copy.14
  107.2 0.7 copy.13
  107.9 0.7 copy.12
  108.6 5.2 %copy.16 = bf16[2048,1280]{1,0:T(8,128)(2,1)} copy(bf16[2048,1280]{1,0:T(8,128)(2,1)} %get-tuple-element.19) | data formatting | bytes 10485760

commit v3 on v2

--- a/solution.py
+++ b/solution.py
@@ -10,33 +10,35 @@
 
 EPS = 1e-06
 
+VMEM_LIMIT = 50 * 1024 * 1024
 ISSUE, RELAY, CROSS, READY, STEP, START, SIDE, PART, END, FINISH = range(10)
 ORDERS = {
     (4, 4, 4): (
         (0, 1, 1, 1),
-        ((0, 0, 0, 0), (0, 1, 0, 1)),
+        ((0, 1, 0, 1), (0, 1, 0, 1)),
         (
             (ISSUE, 0, 0), (ISSUE, 0, 1), (RELAY, 0, 0, 1), (RELAY, 0, 1, 1), (RELAY, 0, 0, 2),
-            (RELAY, 0, 1, 2), (RELAY, 0, 0, 3), (ISSUE, 0, 2), (RELAY, 0, 1, 3), (ISSUE, 0, 3),
-            (RELAY, 0, 2, 1), (READY, 0, 0), (STEP, 0, 0, 0), (STEP, 0, 0, 1), (RELAY, 0, 2, 2),
-            (STEP, 0, 0, 2), (RELAY, 0, 3, 1), (STEP, 0, 0, 3), (RELAY, 0, 2, 3), (START, 0),
-            (READY, 0, 1), (STEP, 0, 1, 0), (RELAY, 0, 3, 2), (STEP, 0, 1, 1), (STEP, 0, 1, 2),
-            (RELAY, 0, 3, 3), (STEP, 0, 1, 3), (PART, 0, 3, 1), (START, 1), (READY, 0, 2),
-            (STEP, 0, 2, 0), (STEP, 0, 2, 1), (STEP, 0, 2, 2), (PART, 0, 2, 1), (PART, 0, 3, 2),
-            (STEP, 0, 2, 3), (SIDE, 1, 0), (START, 2), (SIDE, 1, 3), (READY, 0, 3), (SIDE, 1, 2),
-            (STEP, 0, 3, 0), (SIDE, 1, 1), (STEP, 0, 3, 1), (PART, 1, 3, 1), (STEP, 0, 3, 2),
-            (SIDE, 2, 3), (PART, 1, 2, 1), (END, 0), (SIDE, 2, 0), (STEP, 0, 3, 3),
-            (PART, 1, 3, 2), (PART, 2, 3, 1), (START, 3), (SIDE, 2, 2), (FINISH, 0), (SIDE, 2, 1),
-            (END, 1), (FINISH, 1), (SIDE, 3, 3), (PART, 2, 3, 2), (RELAY, 1, 0, 1),
-            (PART, 2, 2, 1), (SIDE, 3, 0), (SIDE, 3, 2), (RELAY, 1, 0, 2), (RELAY, 1, 1, 1),
-            (PART, 3, 3, 1), (SIDE, 3, 1), (END, 2), (RELAY, 1, 0, 3), (RELAY, 1, 1, 2),
-            (FINISH, 2), (PART, 3, 2, 1), (PART, 3, 3, 2), (RELAY, 1, 1, 3), (CROSS, 1, 1),
-            (RELAY, 1, 2, 1), (END, 3), (READY, 1, 0), (FINISH, 3), (STEP, 1, 0, 0),
-            (STEP, 1, 0, 1), (STEP, 1, 0, 2), (RELAY, 1, 2, 2), (STEP, 1, 0, 3), (READY, 1, 1),
-            (RELAY, 1, 3, 1), (STEP, 1, 1, 0), (RELAY, 1, 2, 3), (STEP, 1, 1, 1), (STEP, 1, 1, 2),
-            (RELAY, 1, 3, 2), (STEP, 1, 1, 3), (CROSS, 1, 3), (READY, 1, 2), (RELAY, 1, 3, 3),
-            (STEP, 1, 2, 0), (STEP, 1, 2, 1), (STEP, 1, 2, 2), (STEP, 1, 2, 3), (READY, 1, 3),
-            (STEP, 1, 3, 0), (STEP, 1, 3, 1), (STEP, 1, 3, 2), (STEP, 1, 3, 3),
+            (RELAY, 0, 1, 2), (RELAY, 0, 0, 3), (ISSUE, 0, 2), (CROSS, 0, 1), (RELAY, 0, 1, 3),
+            (ISSUE, 0, 3), (READY, 0, 0), (STEP, 0, 0, 0), (RELAY, 0, 2, 1), (STEP, 0, 0, 1),
+            (STEP, 0, 0, 2), (STEP, 0, 0, 3), (RELAY, 0, 2, 2), (START, 0), (RELAY, 0, 3, 1),
+            (READY, 0, 1), (RELAY, 0, 2, 3), (STEP, 0, 1, 0), (STEP, 0, 1, 1), (RELAY, 0, 3, 2),
+            (CROSS, 0, 3), (STEP, 0, 1, 2), (RELAY, 0, 3, 3), (STEP, 0, 1, 3), (START, 1),
+            (PART, 0, 3, 1), (READY, 0, 2), (STEP, 0, 2, 0), (STEP, 0, 2, 1), (STEP, 0, 2, 2),
+            (PART, 0, 2, 1), (SIDE, 1, 3), (STEP, 0, 2, 3), (START, 2), (SIDE, 1, 0), (SIDE, 1, 2),
+            (PART, 0, 3, 2), (READY, 0, 3), (STEP, 0, 3, 0), (STEP, 0, 3, 1), (SIDE, 1, 1),
+            (STEP, 0, 3, 2), (SIDE, 2, 0), (PART, 1, 3, 1), (SIDE, 2, 3), (END, 0),
+            (PART, 1, 2, 1), (STEP, 0, 3, 3), (PART, 1, 3, 2), (PART, 2, 3, 1), (SIDE, 2, 2),
+            (START, 3), (FINISH, 0), (SIDE, 2, 1), (END, 1), (FINISH, 1), (PART, 2, 3, 2),
+            (RELAY, 1, 0, 1), (SIDE, 3, 3), (PART, 2, 2, 1), (SIDE, 3, 0), (RELAY, 1, 1, 1),
+            (SIDE, 3, 2), (RELAY, 1, 0, 2), (SIDE, 3, 1), (PART, 3, 3, 1), (END, 2),
+            (RELAY, 1, 1, 2), (RELAY, 1, 0, 3), (FINISH, 2), (PART, 3, 2, 1), (PART, 3, 3, 2),
+            (CROSS, 1, 1), (END, 3), (RELAY, 1, 1, 3), (RELAY, 1, 2, 1), (FINISH, 3),
+            (READY, 1, 0), (STEP, 1, 0, 0), (STEP, 1, 0, 1), (STEP, 1, 0, 2), (RELAY, 1, 2, 2),
+            (STEP, 1, 0, 3), (RELAY, 1, 3, 1), (READY, 1, 1), (RELAY, 1, 2, 3), (STEP, 1, 1, 0),
+            (STEP, 1, 1, 1), (RELAY, 1, 3, 2), (STEP, 1, 1, 2), (CROSS, 1, 3), (STEP, 1, 1, 3),
+            (RELAY, 1, 3, 3), (READY, 1, 2), (STEP, 1, 2, 0), (STEP, 1, 2, 1), (STEP, 1, 2, 2),
+            (STEP, 1, 2, 3), (READY, 1, 3), (STEP, 1, 3, 0), (STEP, 1, 3, 1), (STEP, 1, 3, 2),
+            (STEP, 1, 3, 3),
         ),
     ),
 }
@@ -334,11 +336,11 @@
 
 
 def fused_kernel(
-    plan, key_hbm, value_hbm, query_hbm, rate_ref, gate_ref, up_ref, down_ref, gain_ref,
-    out_hbm, fresh_ref,
-    keys, values, queries, rate, old, new, own, ups, downs, side, updated, weights, acc,
-    squares_old, outs, squares, row, rows_in,
-    load_sem, store_sem,
+    plan, key_hbm, value_hbm, query_hbm, rate_ref, gate_ref, up_ref, down_ref,
+    outs, row_out, fresh_ref,
+    keys, values, rate, old, new, own, ups, downs, side, updated, weights, acc,
+    squares_old, squares, row, rows_in,
+    load_sem,
     line_send, line_recv, cross_send, cross_recv, pass_send, pass_recv,
     part_send, part_recv, side_send, side_recv, row_send, row_recv,
 ):
@@ -350,18 +352,16 @@
     mine = lax.axis_index("head")
     other = z * 2 + 1 - x
 
-    loads = []
     half = 2 * width
+
+    def load(i, p):
+        cut = slice(p * half, (p + 1) * half)
+        src, dst = ((key_hbm, keys), (value_hbm, values), (query_hbm, keys))[i]
+        return pltpu.make_async_copy(src.at[:, cut], dst.at[:, cut], load_sem.at[i, p])
+
     for p in range(heads // 2):
-        cut = slice(p * half, (p + 1) * half)
-        for i, (src, dst) in enumerate(((key_hbm, keys), (value_hbm, values), (query_hbm, queries))):
-            copy = pltpu.make_async_copy(src.at[:, cut], dst.at[:, cut], load_sem.at[i, p])
-            if i < 2:
-                copy.start()
-            loads.append((i, p, copy))
-    for i, p, copy in loads:
-        if i == 2:
-            copy.start()
+        load(0, p).start()
+        load(1, p).start()
 
     barrier = pltpu.get_barrier_semaphore()
     pl.semaphore_signal(barrier, inc=1, device_id={"ctx": other})
@@ -372,7 +372,7 @@
     for t in hops:
         pl.semaphore_signal(barrier, inc=1, device_id={"ctx": lax.rem(z + t, outer) * 2 + x})
 
-    for h in range(heads):
+    def pack_own(h):
         parts = []
         for j, ref in enumerate((gate_ref, up_ref, down_ref)):
             piece = ref[:, h, :].astype(f32)
@@ -380,6 +380,7 @@
             parts.append(plan.move(piece, 0, plan.shifts[j]))
         old[h, me] = plan.pack(*parts).astype(b16)
 
+    pack_own(0)
     pl.semaphore_wait(barrier, plan.peers + len(hops))
 
     sends = []
@@ -418,6 +419,8 @@
         )
 
     def issue(g, h):
+        if g == 0 and h > 0:
+            pack_own(h)
         send(lambda: z < outer - 1, lambda: line_copy(g, h, z, 1))
         send(lambda: z > 0, lambda: line_copy(g, h, z, 0))
         send(None, lambda: cross_copy(g, h, z))
@@ -600,6 +603,8 @@
         lax.fori_loop(0, tokens // step, body, 0)
 
     def start(h):
+        if h % 2:
+            load(2, h // 2).start()
         shift = 64 * (h % 2)
         for b in range(n):
             parts = [
@@ -614,7 +619,7 @@
         def body(i, _):
             at_steps(i, slots)
             span = pl.ds(pl.multiple_of(i * step, step), step)
-            query = queries[span, cut]
+            query = keys[span, cut]
             gate = dot(query, weights[0], 1, 1)
             up = dot(query, weights[1], 1, 1)
             mixed = (jax.nn.silu(gate) * up).astype(b16)
@@ -629,19 +634,20 @@
             total = part[:, :128]
             for c in range(128, window, 128):
                 total = total + part[:, c : c + 128]
-            squares[span, :] = total if h == 0 else squares[span, :] + total
+            if h > 0:
+                total = squares[span, :] + total
+            if h < heads - 1:
+                squares[span, :] = total
+            else:
+                row[:, span] = jnp.sum(total.T, axis=0, keepdims=True)
             return 0
 
         lax.fori_loop(0, tokens // step, body, 0)
 
-    def loaded(h, kinds):
+    def ready(g, h):
         if h % 2 == 0:
-            for i, p, copy in loads:
-                if p == h // 2 and i in kinds:
-                    copy.wait()
-
-    def ready(g, h):
-        loaded(h, (2,) if g else (0, 1))
+            for i in (2,) if g else (0, 1):
+                load(i, h // 2).wait()
         arrived(g, h)
         (prepare_new if g else prepare_old)(h)
 
@@ -649,14 +655,17 @@
         ISSUE: issue, RELAY: relay, CROSS: cross, READY: ready, START: start, SIDE: reduce_beside,
         PART: reduce_relay, END: reduce_end, FINISH: renew,
     }
-    turned = rate_ref[...]
-    if heads < 8:
-        turned = jnp.concatenate([turned, jnp.zeros((8 - heads, tokens), f32)], axis=0)
-    rate[...] = turned.T
+    def turn_rates():
+        turned = rate_ref[...]
+        if heads < 8:
+            turned = jnp.concatenate([turned, jnp.zeros((8 - heads, tokens), f32)], axis=0)
+        rate[...] = turned.T
 
     order = list(order)
     while order:
         event = order.pop(0)
+        if event == (RELAY, 0, 0, 1):
+            turn_rates()
         if event[0] != READY:
             handlers[event[0]](*event[1:])
             continue
@@ -669,8 +678,6 @@
             order.pop(0)
         (apply_head if event[1] else grads)(event[2], slots)
 
-    row[...] = jnp.sum(squares[...].T, axis=0, keepdims=True)
-
     def row_copy(t):
         return pltpu.make_async_remote_copy(
             src_ref=row, dst_ref=rows_in.at[t - 1],
@@ -684,30 +691,52 @@
     for t in range(1, plan.peers):
         row_copy(t).wait_recv()
         total = total + rows_in[t - 1]
-    row_scale = lax.rsqrt(total / plan.width_all + EPS)
-    column = jnp.broadcast_to(row_scale, (128, tokens)).T
-    squares[...] = column
-
-    def finish(i):
-        span = pl.ds(pl.multiple_of(i * step, step), step)
-        return pltpu.make_async_copy(keys.at[span], out_hbm.at[span], store_sem.at[i])
-
-    def body(i, _):
-        span = pl.ds(pl.multiple_of(i * step, step), step)
-        for c in range(0, heads * width, 128):
-            scaled = outs[span, c : c + 128] * squares[span, :] * gain_ref[:, c : c + 128]
-            keys[span, c : c + 128] = scaled.astype(b16)
-        finish(i).start()
-        return 0
-
-    lax.fori_loop(0, tokens // step, body, 0)
+    row_out[...] = lax.rsqrt(total / plan.width_all + EPS)
     for done in sends:
         done()
+
+
+def finish_kernel(step, outs_ref, row_ref, gain_ref, fresh_ref, out_hbm, gate_ref, up_ref, down_ref, staged, sem):
+    tokens, width = outs_ref.shape
+
+    def store(i):
+        span = pl.ds(i * step, step)
+        return pltpu.make_async_copy(staged.at[span], out_hbm.at[span], sem.at[i])
+
     for i in range(tokens // step):
-        finish(i).wait()
-
-
-def fused(n, peers, width_all, keys, values, queries, rates, w_gate, w_up, w_down, gain):
+        span = slice(i * step, (i + 1) * step)
+        scale = jnp.broadcast_to(row_ref[:, span], (128, step)).T
+        for c in range(0, width, 128):
+            cut = slice(c, c + 128)
+            staged[span, cut] = (outs_ref[span, cut] * scale * gain_ref[cut][None]).astype(staged.dtype)
+        store(i).start()
+    for j, ref in enumerate((gate_ref, up_ref, down_ref)):
+        heads = [fresh_ref[j, h].astype(jnp.float32) for h in range(fresh_ref.shape[1])]
+        ref[...] = jnp.stack(heads, axis=1).astype(ref.dtype)
+    for i in range(tokens // step):
+        store(i).wait()
+
+
+def finish(outs, row, gain, fresh):
+    rows, width = outs.shape
+    units, heads = fresh.shape[2], fresh.shape[1]
+    weight = jax.ShapeDtypeStruct((units, heads, fresh.shape[3]), fresh.dtype)
+    step = 256
+    return pl.pallas_call(
+        functools.partial(finish_kernel, step),
+        out_shape=(jax.ShapeDtypeStruct(outs.shape, jnp.bfloat16),) + (weight,) * 3,
+        in_specs=vmem(4),
+        out_specs=(pl.BlockSpec(memory_space=pl.ANY),) + tuple(vmem(3)),
+        scratch_shapes=[
+            pltpu.VMEM(outs.shape, jnp.bfloat16),
+            pltpu.SemaphoreType.DMA((rows // step,)),
+        ],
+        compiler_params=pltpu.CompilerParams(vmem_limit_bytes=32 * 1024 * 1024),
+        name="finish_rows",
+    )(outs, row, gain, fresh)
+
+
+def fused(n, peers, width_all, keys, values, queries, rates, w_gate, w_up, w_down):
     rows = keys.shape[0]
     units, heads, width = w_gate.shape
     plan = Plan(n, peers, rows, units, heads, width, width_all)
@@ -719,13 +748,13 @@
     return pl.pallas_call(
         functools.partial(fused_kernel, plan),
         out_shape=(
-            jax.ShapeDtypeStruct(keys.shape, b16),
-            jax.ShapeDtypeStruct((3, heads, units, width), b16),
+            pltpu.VMEM(keys.shape, f32),
+            pltpu.VMEM((1, rows), f32),
+            pltpu.VMEM((3, heads, units, width), b16),
         ),
-        in_specs=[hbm] * 3 + vmem(5),
-        out_specs=(hbm, vmem(1)[0]),
+        in_specs=[hbm] * 3 + vmem(4),
+        out_specs=tuple(vmem(3)),
         scratch_shapes=[
-            pltpu.VMEM(keys.shape, b16),
             pltpu.VMEM(keys.shape, b16),
             pltpu.VMEM(keys.shape, b16),
             pltpu.VMEM((rows, 8), f32),
@@ -739,12 +768,10 @@
             pltpu.VMEM((3, n * units, plan.window), b16),
             pltpu.VMEM((3, n * units, plan.window), f32),
             pltpu.VMEM((3 * heads, plan.window), f32),
-            pltpu.VMEM(keys.shape, f32),
             pltpu.VMEM((rows, 128), f32),
             pltpu.VMEM((1, rows), f32),
             pltpu.VMEM((peers - 1, 1, rows), f32),
             dma((3, heads // 2)),
-            dma((rows // plan.step,)),
             dma((2, heads, 2, outer)),
             dma((2, heads, outer)),
             dma((2, heads, outer)),
@@ -759,10 +786,10 @@
             dma((peers - 1,)),
         ],
         compiler_params=pltpu.CompilerParams(
-            collective_id=2, has_side_effects=True, vmem_limit_bytes=67043328
+            collective_id=2, has_side_effects=True, vmem_limit_bytes=VMEM_LIMIT
         ),
         name="fused_layer",
-    )(keys, values, queries, rates.T, w_gate, w_up, w_down, gain[None])
+    )(keys, values, queries, rates.T, w_gate, w_up, w_down)
 
 
 def per_device(n, peers, width_all, keys, values, queries, rates, w_gate, w_up, w_down, gain):
@@ -770,11 +797,10 @@
     units, heads, width = w_gate.shape
     f32 = jnp.float32
     if fits(n, rows, units, heads, width):
-        output, fresh = fused(
-            n, peers, width_all, keys, values, queries, rates, w_gate, w_up, w_down, gain
+        outs, row, fresh = fused(
+            n, peers, width_all, keys, values, queries, rates, w_gate, w_up, w_down
         )
-        fresh = fresh.transpose(0, 2, 1, 3)
-        return (output, fresh[0], fresh[1], fresh[2])
+        return finish(outs, row, gain, fresh)
     own = jnp.stack([w_gate, w_up, w_down]).transpose(0, 2, 1, 3)
     own = own.reshape(3 * heads, units, width)
     full = gather(own, n).transpose(1, 3, 0, 2)

time: 114 us -> 104 us (0.912)
  local copies, waits for them, and re-layouts: 9.62 us -> 0.01 us
    unnamed x4 -> x2, local copies, waits for them, and re-layouts: 7.27 us -> 0.01 us
    broadcast_in_dim x1 -> x0, local copies, waits for them, and re-layouts: 1.29 us -> none  [fused(): gain[None]]
    pallas_call x1 -> x2, Pallas kernels: 104 us -> 103 us  [the longest x1 99.3 us: fused(): pl.pallas_call(functools.partial(fused_kernel, plan), out_shape=(pltpu.VM...]
where the time goes in v3:
time: 104 us
  Pallas kernels  103 us (99%)
    pallas_call x1, Pallas kernels, fused(): pl.pallas_call(functools.partial(fused_kernel, plan), out_shape=(pltpu.VM...  99.3 us
    pallas_call x1, Pallas kernels, finish(): pl.pallas_call(functools.partial(finish_kernel, step), out_shape=(jax.Sha...  3.36 us

profile of v3, /device:TPU:0, one launch (start us, length us, event | category | flops | bytes accessed | tf_op | source)
XLA Modules:
  0.0 103.5 jit_solution(13604015306659904700)
XLA Ops:
  0.6 0.0 copy-start
  0.6 99.3 %fused_layer.1 = (f32[2048,1280]{1,0:T(8,128)S(1)}, f32[1,2048]{1,0:T(1,128)S(1)}, bf16[3,4,40,320]{3,2,1,0:T(8,128)(2,1)S(1)}) custom-call(bf16[2048,1280]{1,0:T(8,128)(2,1)} %key_hbm.1, bf16[2048,1280]{1,0:T(8,128)(2,1)} %value_hbm.1, bf16[2048,1280]{1,0:T(8,128)(2,1)} %query_hbm.1, f32[4,2048]{1,0:T(4,128)} %bitcast.1, bf16[40,4,320]{2,1,0:T(4,128)(2,1)} %gate_ref.1, ...), custom_call_target="tpu_custom_call" | custom-call | tf_op jit(solution)/shard_map/fused_layer/pallas_call | solution.py:748
  100.0 0.0 copy-done
  100.0 3.4 %finish_rows.1 = (bf16[2048,1280]{1,0:T(8,128)(2,1)}, bf16[40,4,320]{2,1,0:T(4,128)(2,1)}, bf16[40,4,320]{2,1,0:T(4,128)(2,1)}, bf16[40,4,320]{2,1,0:T(4,128)(2,1)}) custom-call(f32[2048,1280]{1,0:T(8,128)S(1)} %get-tuple-element.7.outs_ref, f32[1,2048]{1,0:T(1,128)S(1)} %get-tuple-element.8.row_ref, f32[1280]{0:T(1024)S(1)} %copy-done, ...), custom_call_target="tpu_custom_call" | custom-call | tf_op jit(solution)/shard_map/finish_rows/pallas_call | solution.py:725
Async XLA Ops:
  0.6 99.4 %copy-start = (f32[1280]{0:T(1024)S(1)}, f32[1280]{0:T(1024)}, u32[]{:S(2)}) copy-start(f32[1280]{0:T(1024)} %gain_ref.1) | copy-start | bytes 15364

commit v4 on v3

--- a/solution.py
+++ b/solution.py
@@ -11,34 +11,49 @@
 EPS = 1e-06
 
 VMEM_LIMIT = 50 * 1024 * 1024
+STEPS = (1024, 1024)
 ISSUE, RELAY, CROSS, READY, STEP, START, SIDE, PART, END, FINISH = range(10)
 ORDERS = {
-    (4, 4, 4): (
-        (0, 1, 1, 1),
-        ((0, 1, 0, 1), (0, 1, 0, 1)),
+    (4, 4, 2048): (
+        ((0, 0), (0, 1), (1, 1), (1, 1)),
+        (((0, 1), (0, 1), (0, 1), (0, 1)), ((0, 1), (0, 1), (0, 1), (2, 2))),
         (
-            (ISSUE, 0, 0), (ISSUE, 0, 1), (RELAY, 0, 0, 1), (RELAY, 0, 1, 1), (RELAY, 0, 0, 2),
-            (RELAY, 0, 1, 2), (RELAY, 0, 0, 3), (ISSUE, 0, 2), (CROSS, 0, 1), (RELAY, 0, 1, 3),
-            (ISSUE, 0, 3), (READY, 0, 0), (STEP, 0, 0, 0), (RELAY, 0, 2, 1), (STEP, 0, 0, 1),
-            (STEP, 0, 0, 2), (STEP, 0, 0, 3), (RELAY, 0, 2, 2), (START, 0), (RELAY, 0, 3, 1),
-            (READY, 0, 1), (RELAY, 0, 2, 3), (STEP, 0, 1, 0), (STEP, 0, 1, 1), (RELAY, 0, 3, 2),
-            (CROSS, 0, 3), (STEP, 0, 1, 2), (RELAY, 0, 3, 3), (STEP, 0, 1, 3), (START, 1),
-            (PART, 0, 3, 1), (READY, 0, 2), (STEP, 0, 2, 0), (STEP, 0, 2, 1), (STEP, 0, 2, 2),
-            (PART, 0, 2, 1), (SIDE, 1, 3), (STEP, 0, 2, 3), (START, 2), (SIDE, 1, 0), (SIDE, 1, 2),
-            (PART, 0, 3, 2), (READY, 0, 3), (STEP, 0, 3, 0), (STEP, 0, 3, 1), (SIDE, 1, 1),
-            (STEP, 0, 3, 2), (SIDE, 2, 0), (PART, 1, 3, 1), (SIDE, 2, 3), (END, 0),
-            (PART, 1, 2, 1), (STEP, 0, 3, 3), (PART, 1, 3, 2), (PART, 2, 3, 1), (SIDE, 2, 2),
-            (START, 3), (FINISH, 0), (SIDE, 2, 1), (END, 1), (FINISH, 1), (PART, 2, 3, 2),
-            (RELAY, 1, 0, 1), (SIDE, 3, 3), (PART, 2, 2, 1), (SIDE, 3, 0), (RELAY, 1, 1, 1),
-            (SIDE, 3, 2), (RELAY, 1, 0, 2), (SIDE, 3, 1), (PART, 3, 3, 1), (END, 2),
-            (RELAY, 1, 1, 2), (RELAY, 1, 0, 3), (FINISH, 2), (PART, 3, 2, 1), (PART, 3, 3, 2),
-            (CROSS, 1, 1), (END, 3), (RELAY, 1, 1, 3), (RELAY, 1, 2, 1), (FINISH, 3),
-            (READY, 1, 0), (STEP, 1, 0, 0), (STEP, 1, 0, 1), (STEP, 1, 0, 2), (RELAY, 1, 2, 2),
-            (STEP, 1, 0, 3), (RELAY, 1, 3, 1), (READY, 1, 1), (RELAY, 1, 2, 3), (STEP, 1, 1, 0),
-            (STEP, 1, 1, 1), (RELAY, 1, 3, 2), (STEP, 1, 1, 2), (CROSS, 1, 3), (STEP, 1, 1, 3),
-            (RELAY, 1, 3, 3), (READY, 1, 2), (STEP, 1, 2, 0), (STEP, 1, 2, 1), (STEP, 1, 2, 2),
-            (STEP, 1, 2, 3), (READY, 1, 3), (STEP, 1, 3, 0), (STEP, 1, 3, 1), (STEP, 1, 3, 2),
-            (STEP, 1, 3, 3),
+            (ISSUE, 0, 0, 0), (ISSUE, 0, 0, 1), (ISSUE, 0, 1, 0), (ISSUE, 0, 1, 1),
+            (RELAY, 0, 0, 0, 1), (RELAY, 0, 0, 1, 1), (RELAY, 0, 1, 0, 1), (CROSS, 0, 0, 1),
+            (RELAY, 0, 0, 0, 2), (RELAY, 0, 0, 1, 2), (RELAY, 0, 1, 1, 1), (ISSUE, 0, 2, 0),
+            (ISSUE, 0, 2, 1), (CROSS, 0, 1, 1), (RELAY, 0, 0, 0, 3), (RELAY, 0, 0, 1, 3),
+            (RELAY, 0, 1, 1, 2), (RELAY, 0, 1, 0, 2), (ISSUE, 0, 3, 0), (ISSUE, 0, 3, 1),
+            (READY, 0, 0), (RELAY, 0, 2, 0, 1), (STEP, 0, 0, 0), (RELAY, 0, 1, 1, 3),
+            (RELAY, 0, 1, 0, 3), (RELAY, 0, 2, 1, 1), (CROSS, 0, 2, 1), (STEP, 0, 0, 1),
+            (CROSS, 0, 3, 1), (START, 0), (RELAY, 0, 2, 0, 2), (RELAY, 0, 2, 1, 2),
+            (RELAY, 0, 3, 0, 1), (READY, 0, 1), (STEP, 0, 1, 0), (RELAY, 0, 2, 0, 3),
+            (RELAY, 0, 2, 1, 3), (STEP, 0, 1, 1), (RELAY, 0, 3, 0, 2), (RELAY, 0, 3, 0, 3),
+            (RELAY, 0, 3, 1, 1), (START, 1), (READY, 0, 2), (STEP, 0, 2, 0), (RELAY, 0, 3, 1, 2),
+            (RELAY, 0, 3, 1, 3), (PART, 0, 0, 3, 1), (PART, 0, 0, 2, 1), (STEP, 0, 2, 1),
+            (START, 2), (SIDE, 1, 1, 1), (PART, 0, 1, 3, 1), (SIDE, 1, 1, 2), (SIDE, 1, 1, 3),
+            (PART, 0, 0, 3, 2), (SIDE, 1, 1, 0), (PART, 0, 1, 2, 1), (READY, 0, 3),
+            (STEP, 0, 3, 0), (PART, 0, 1, 3, 2), (SIDE, 2, 0, 3), (END, 0, 0), (SIDE, 2, 0, 2),
+            (SIDE, 2, 0, 0), (END, 0, 1), (SIDE, 2, 0, 1), (PART, 1, 0, 3, 1), (PART, 1, 0, 2, 1),
+            (STEP, 0, 3, 1), (START, 3), (PART, 1, 1, 3, 1), (FINISH, 0, 0), (FINISH, 0, 1),
+            (SIDE, 2, 1, 2), (PART, 1, 1, 2, 1), (SIDE, 2, 1, 0), (PART, 1, 0, 3, 2),
+            (PART, 2, 0, 3, 1), (PART, 2, 0, 2, 1), (SIDE, 2, 1, 3), (SIDE, 2, 1, 1),
+            (PART, 1, 1, 3, 2), (END, 1, 0), (RELAY, 1, 0, 0, 1), (RELAY, 1, 0, 1, 1),
+            (SIDE, 3, 0, 3), (END, 1, 1), (FINISH, 1, 1), (SIDE, 3, 0, 0), (PART, 2, 0, 3, 2),
+            (SIDE, 3, 1, 0), (SIDE, 3, 0, 1), (SIDE, 3, 1, 3), (RELAY, 1, 0, 0, 2),
+            (RELAY, 1, 0, 0, 3), (PART, 2, 1, 3, 1), (SIDE, 3, 0, 2), (PART, 2, 1, 2, 1),
+            (RELAY, 1, 0, 1, 2), (END, 2, 0), (FINISH, 2, 0), (SIDE, 3, 1, 2), (RELAY, 1, 1, 1, 1),
+            (FINISH, 1, 0), (RELAY, 1, 0, 1, 3), (PART, 3, 0, 3, 1), (PART, 2, 1, 3, 2),
+            (END, 2, 1), (FINISH, 2, 1), (RELAY, 1, 1, 1, 2), (PART, 3, 1, 3, 1),
+            (RELAY, 1, 2, 0, 1), (PART, 3, 0, 3, 2), (PART, 3, 0, 2, 1), (RELAY, 1, 1, 0, 1),
+            (SIDE, 3, 1, 1), (PART, 3, 1, 3, 2), (CROSS, 1, 0, 1), (RELAY, 1, 2, 1, 1),
+            (PART, 3, 1, 2, 1), (RELAY, 1, 2, 0, 2), (END, 3, 0), (RELAY, 1, 1, 0, 2),
+            (FINISH, 3, 0), (RELAY, 1, 2, 1, 2), (RELAY, 1, 1, 0, 3), (RELAY, 1, 1, 1, 3),
+            (CROSS, 1, 1, 1), (END, 3, 1), (FINISH, 3, 1), (READY, 1, 0), (STEP, 1, 0, 0),
+            (RELAY, 1, 2, 0, 3), (RELAY, 1, 3, 0, 1), (RELAY, 1, 3, 0, 2), (CROSS, 1, 2, 1),
+            (RELAY, 1, 2, 1, 3), (STEP, 1, 0, 1), (READY, 1, 1), (RELAY, 1, 3, 0, 3),
+            (STEP, 1, 1, 0), (RELAY, 1, 3, 1, 1), (RELAY, 1, 3, 1, 2), (RELAY, 1, 3, 1, 3),
+            (STEP, 1, 1, 1), (READY, 1, 2), (STEP, 1, 2, 0), (STEP, 1, 2, 1), (READY, 1, 3),
+            (STEP, 1, 3, 0), (STEP, 1, 3, 1),
         ),
     ),
 }
@@ -300,9 +315,9 @@
         and heads % 2 == 0
         and heads <= 8
         and width % 128 == 64
-        and rows % 512 == 0
+        and rows % max(STEPS) == 0
         and rows * heads * width <= 2048 * 1280
-        and (n // inner, heads, rows // 512) in ORDERS
+        and (n // inner, heads, rows) in ORDERS
     )
 
 
@@ -312,7 +327,7 @@
         self.heads, self.width, self.width_all = heads, width, width_all
         self.inner = 2
         self.outer = n // 2
-        self.step = 512
+        self.step, self.long = STEPS
         self.window = width + 64
         self.packed = 2 * width + self.window
         self.starts = (0, width - 64, 2 * width)
@@ -346,7 +361,7 @@
 ):
     f32, b16 = jnp.float32, jnp.bfloat16
     n, outer, heads, units, width = plan.n, plan.outer, plan.heads, plan.units, plan.width
-    window, step, tokens = plan.window, plan.step, plan.rows
+    window, step, long, tokens = plan.window, plan.step, plan.long, plan.rows
     me = lax.axis_index("ctx")
     z, x = me // 2, lax.rem(me, 2)
     mine = lax.axis_index("head")
@@ -368,8 +383,7 @@
     for t in range(1, plan.peers):
         pl.semaphore_signal(barrier, inc=1, device_id={"head": lax.rem(mine + t, plan.peers)})
 
-    hops = sorted({1, outer - 1})
-    for t in hops:
+    for t in range(1, outer):
         pl.semaphore_signal(barrier, inc=1, device_id={"ctx": lax.rem(z + t, outer) * 2 + x})
 
     def pack_own(h):
@@ -381,10 +395,10 @@
         old[h, me] = plan.pack(*parts).astype(b16)
 
     pack_own(0)
-    pl.semaphore_wait(barrier, plan.peers + len(hops))
+    pl.semaphore_wait(barrier, plan.peers + outer - 1)
 
     sends = []
-    side_first, passing, order = ORDERS[outer, heads, tokens // step]
+    side_first, passing, order = ORDERS[outer, heads, tokens]
 
     def send(when, make):
         def start():
@@ -400,150 +414,194 @@
             pl.when(when())(start)
             sends.append(lambda: pl.when(when())(finish))
 
-    def line_copy(g, h, origin, up):
+    parts = 2
+    share = plan.packed // parts
+    lanes = lambda p: slice(p * share, (p + 1) * share)
+
+    def line_copy(g, h, p, origin, up):
         buf = (old, new)[g]
         block = origin * 2 + x
         return pltpu.make_async_remote_copy(
-            src_ref=buf.at[h, block], dst_ref=buf.at[h, block],
-            send_sem=line_send.at[g, h, up, origin], recv_sem=line_recv.at[g, h, origin],
+            src_ref=buf.at[h, block, :, lanes(p)], dst_ref=buf.at[h, block, :, lanes(p)],
+            send_sem=line_send.at[g, h * parts + p, up, origin], recv_sem=line_recv.at[g, h * parts + p, origin],
             device_id={"ctx": me + (2 if up else -2)},
         )
 
-    def cross_copy(g, h, origin):
+    def cross_copy(g, h, p, origin):
         buf = (old, new)[g]
         block = origin * 2 + x
         return pltpu.make_async_remote_copy(
-            src_ref=buf.at[h, block], dst_ref=buf.at[h, block],
-            send_sem=cross_send.at[g, h, origin], recv_sem=cross_recv.at[g, h, origin],
+            src_ref=buf.at[h, block, :, lanes(p)], dst_ref=buf.at[h, block, :, lanes(p)],
+            send_sem=cross_send.at[g, h * parts + p, origin], recv_sem=cross_recv.at[g, h * parts + p, origin],
             device_id={"ctx": other},
         )
 
-    def issue(g, h):
-        if g == 0 and h > 0:
+    def far_copy(g, h, p, to):
+        buf = (old, new)[g]
+        return pltpu.make_async_remote_copy(
+            src_ref=buf.at[h, me, :, lanes(p)], dst_ref=buf.at[h, me, :, lanes(p)],
+            send_sem=line_send.at[g, h * parts + p, 0, to], recv_sem=line_recv.at[g, h * parts + p, z],
+            device_id={"ctx": to * 2 + x},
+        )
+
+    def issue(g, h, p):
+        if g == 0 and h > 0 and p == 0:
             pack_own(h)
-        send(lambda: z < outer - 1, lambda: line_copy(g, h, z, 1))
-        send(lambda: z > 0, lambda: line_copy(g, h, z, 0))
-        send(None, lambda: cross_copy(g, h, z))
-
-    def relay(g, h, d):
-        whole = d > 1 or not passing[g][h]
+        if passing[g][h][p] > 1:
+            for d in range(outer - 1, 0, -1):
+                send(lambda d=d: z + d < outer, lambda d=d: far_copy(g, h, p, z + d))
+                send(lambda d=d: z >= d, lambda d=d: far_copy(g, h, p, z - d))
+            send(None, lambda: cross_copy(g, h, p, z))
+            return
+        send(lambda: z < outer - 1, lambda: line_copy(g, h, p, z, 1))
+        send(lambda: z > 0, lambda: line_copy(g, h, p, z, 0))
+        send(None, lambda: cross_copy(g, h, p, z))
+
+    def relay(g, h, p, d):
+        whole = d > 1 or not passing[g][h][p] & 1
+        onward = passing[g][h][p] < 2
 
         @pl.when(z >= d)
         def _():
-            line_copy(g, h, z - d, 1).wait_recv()
-
-        send(lambda: (z >= d) & (z < outer - 1), lambda: line_copy(g, h, z - d, 1))
+            line_copy(g, h, p, z - d, 1).wait_recv()
+
+        if onward:
+            send(lambda: (z >= d) & (z < outer - 1), lambda: line_copy(g, h, p, z - d, 1))
         if whole:
-            send(lambda: z >= d, lambda: cross_copy(g, h, z - d))
+            send(lambda: z >= d, lambda: cross_copy(g, h, p, z - d))
 
         @pl.when(z + d < outer)
         def _():
-            line_copy(g, h, z + d, 0).wait_recv()
-
-        send(lambda: (z + d < outer) & (z > 0), lambda: line_copy(g, h, z + d, 0))
+            line_copy(g, h, p, z + d, 0).wait_recv()
+
+        if onward:
+            send(lambda: (z + d < outer) & (z > 0), lambda: line_copy(g, h, p, z + d, 0))
         if whole:
-            send(lambda: z + d < outer, lambda: cross_copy(g, h, z + d))
-
-    def pass_copy(g, h, up):
+            send(lambda: z + d < outer, lambda: cross_copy(g, h, p, z + d))
+
+    def pass_copy(g, h, p, up):
         buf = (old, new)[g]
         return pltpu.make_async_remote_copy(
-            src_ref=buf.at[h, other], dst_ref=buf.at[h, other],
-            send_sem=pass_send.at[g, h, up], recv_sem=pass_recv.at[g, h, up],
+            src_ref=buf.at[h, other, :, lanes(p)], dst_ref=buf.at[h, other, :, lanes(p)],
+            send_sem=pass_send.at[g, h * parts + p, up], recv_sem=pass_recv.at[g, h * parts + p, up],
             device_id={"ctx": me + (2 if up else -2)},
         )
 
-    def cross(g, h):
-        cross_copy(g, h, z).wait_recv()
-        send(lambda: z < outer - 1, lambda: pass_copy(g, h, 1))
-        send(lambda: z > 0, lambda: pass_copy(g, h, 0))
-
-    def arrived(g, h):
-        if not passing[g][h]:
+    def cross(g, h, p):
+        cross_copy(g, h, p, z).wait_recv()
+        send(lambda: z < outer - 1, lambda: pass_copy(g, h, p, 1))
+        send(lambda: z > 0, lambda: pass_copy(g, h, p, 0))
+
+    def arrived(g, h, p):
+        if not passing[g][h][p] & 1:
             for o in range(outer):
-                cross_copy(g, h, o).wait_recv()
+                cross_copy(g, h, p, o).wait_recv()
             return
         for o in range(outer):
-            pl.when((o > z + 1) | (o < z - 1))(lambda: cross_copy(g, h, o).wait_recv())
-        pl.when(z > 0)(lambda: pass_copy(g, h, 1).wait_recv())
-        pl.when(z < outer - 1)(lambda: pass_copy(g, h, 0).wait_recv())
-
-    def part_copy(h, up, to):
+            pl.when((o > z + 1) | (o < z - 1))(lambda: cross_copy(g, h, p, o).wait_recv())
+        pl.when(z > 0)(lambda: pass_copy(g, h, p, 1).wait_recv())
+        pl.when(z < outer - 1)(lambda: pass_copy(g, h, p, 0).wait_recv())
+
+    def part_copy(h, p, up, to):
         buf = (downs, ups)[up]
-        first, count = (to * 2 + x, 1) if side_first[h] else (to * 2, 2)
+        first, count = (to * 2 + x, 1) if side_first[h][p] else (to * 2, 2)
         return pltpu.make_async_remote_copy(
-            src_ref=own.at[h, pl.ds(first, count)], dst_ref=buf.at[h, to, pl.ds(0, count)],
-            send_sem=part_send.at[h, up, to], recv_sem=part_recv.at[h, up, to],
+            src_ref=own.at[h, pl.ds(first, count), :, lanes(p)], dst_ref=buf.at[h, to, pl.ds(0, count), :, lanes(p)],
+            send_sem=part_send.at[h * parts + p, up, to], recv_sem=part_recv.at[h * parts + p, up, to],
             device_id={"ctx": me + (2 if up else -2)},
         )
 
-    def add_part(h, up, to):
+    def add_part(h, p, up, to):
         buf = (downs, ups)[up]
-        part_copy(h, up, to).wait_recv()
-        for c in range(1 if side_first[h] else 2):
-            block = to * 2 + (x if side_first[h] else c)
-            total = own[h, block].astype(f32) + buf[h, to, c].astype(f32)
-            own[h, block] = total.astype(b16)
-
-    def side_copy(h, to):
+        part_copy(h, p, up, to).wait_recv()
+        for c in range(1 if side_first[h][p] else 2):
+            block = to * 2 + (x if side_first[h][p] else c)
+            total = own[h, block, :, lanes(p)].astype(f32) + buf[h, to, c, :, lanes(p)].astype(f32)
+            own[h, block, :, lanes(p)] = total.astype(b16)
+
+    def far_part(h, p, to, slot):
         return pltpu.make_async_remote_copy(
-            src_ref=own.at[h, to * 2 + 1 - x], dst_ref=side.at[h, to if side_first[h] else 0],
-            send_sem=side_send.at[h, to], recv_sem=side_recv.at[h, to],
+            src_ref=own.at[h, to * 2 + x, :, lanes(p)], dst_ref=ups.at[h, slot, 0, :, lanes(p)],
+            send_sem=part_send.at[h * parts + p, 0, to], recv_sem=part_recv.at[h * parts + p, 1, slot],
+            device_id={"ctx": to * 2 + x},
+        )
+
+    def side_copy(h, p, to):
+        return pltpu.make_async_remote_copy(
+            src_ref=own.at[h, to * 2 + 1 - x, :, lanes(p)], dst_ref=side.at[h, to if side_first[h][p] else 0, :, lanes(p)],
+            send_sem=side_send.at[h * parts + p, to], recv_sem=side_recv.at[h * parts + p, to],
             device_id={"ctx": other},
         )
 
-    def reduce_start(h):
-        if side_first[h]:
+    def reduce_start(h, p):
+        if side_first[h][p]:
             for i in range(outer):
-                send(None, functools.partial(side_copy, h, i // 2 if i % 2 else outer - 1 - i // 2))
+                send(None, functools.partial(side_copy, h, p, i // 2 if i % 2 else outer - 1 - i // 2))
             return
         for to in range(outer - 1, 0, -1):
-            send(lambda: z == 0, functools.partial(part_copy, h, 1, to))
-            send(lambda: z == outer - 1, functools.partial(part_copy, h, 0, outer - 1 - to))
-
-    def reduce_beside(h, to):
-        side_copy(h, to).wait_recv()
-        total = own[h, to * 2 + x].astype(f32) + side[h, to].astype(f32)
-        own[h, to * 2 + x] = total.astype(b16)
+            send(lambda: z == 0, functools.partial(part_copy, h, p, 1, to))
+            send(lambda: z == outer - 1, functools.partial(part_copy, h, p, 0, outer - 1 - to))
+
+    def reduce_beside(h, p, to):
+        side_copy(h, p, to).wait_recv()
+        total = own[h, to * 2 + x, :, lanes(p)].astype(f32) + side[h, to, :, lanes(p)].astype(f32)
+        own[h, to * 2 + x, :, lanes(p)] = total.astype(b16)
+        if side_first[h][p] > 1:
+            send(lambda: z != to, lambda: far_part(h, p, to, z))
+            return
         if to > 0:
-            send(lambda: z == 0, lambda: part_copy(h, 1, to))
+            send(lambda: z == 0, lambda: part_copy(h, p, 1, to))
         if to < outer - 1:
-            send(lambda: z == outer - 1, lambda: part_copy(h, 0, to))
-
-    def reduce_relay(h, to, d):
+            send(lambda: z == outer - 1, lambda: part_copy(h, p, 0, to))
+
+    def reduce_relay(h, p, to, d):
         back = outer - 1 - to
 
         @pl.when(z == d)
         def _():
-            add_part(h, 1, to)
-
-        send(lambda: z == d, lambda: part_copy(h, 1, to))
+            add_part(h, p, 1, to)
+
+        send(lambda: z == d, lambda: part_copy(h, p, 1, to))
 
         @pl.when(z == outer - 1 - d)
         def _():
-            add_part(h, 0, back)
-
-        send(lambda: z == outer - 1 - d, lambda: part_copy(h, 0, back))
-
-    def reduce_end(h):
+            add_part(h, p, 0, back)
+
+        send(lambda: z == outer - 1 - d, lambda: part_copy(h, p, 0, back))
+
+    def reduce_end(h, p):
+        if side_first[h][p] > 1:
+            total = own[h, me, :, lanes(p)].astype(f32)
+            for d in range(1, outer):
+                source = lax.rem(z + d, outer)
+                far_part(h, p, source, source).wait_recv()
+                total = total + ups[h, source, 0, :, lanes(p)].astype(f32)
+            updated[h, :, lanes(p)] = total
+            return
+
         @pl.when(z > 0)
         def _():
-            add_part(h, 1, z)
+            add_part(h, p, 1, z)
 
         @pl.when(z < outer - 1)
         def _():
-            add_part(h, 0, z)
-
-        if not side_first[h]:
-            send(None, lambda: side_copy(h, z))
-
-    def renew(h):
-        total = own[h, me].astype(f32) + old[h, me].astype(f32)
-        if not side_first[h]:
-            side_copy(h, z).wait_recv()
-            total = total + side[h, 0].astype(f32)
-        updated[h] = total
-        new[h, me] = total.astype(b16)
-        issue(1, h)
+            add_part(h, p, 0, z)
+
+        if not side_first[h][p]:
+            send(None, lambda: side_copy(h, p, z))
+
+    def renew(h, p):
+        if side_first[h][p] > 1:
+            total = updated[h, :, lanes(p)]
+        else:
+            total = own[h, me, :, lanes(p)].astype(f32)
+        total = total + old[h, me, :, lanes(p)].astype(f32)
+        if not side_first[h][p]:
+            side_copy(h, p, z).wait_recv()
+            total = total + side[h, 0, :, lanes(p)].astype(f32)
+        updated[h, :, lanes(p)] = total
+        new[h, me, :, lanes(p)] = total.astype(b16)
+        issue(1, h, p)
 
     def pieces(g, h, j):
         buf = (old, new)[g]
@@ -607,23 +665,24 @@
             load(2, h // 2).start()
         shift = 64 * (h % 2)
         for b in range(n):
-            parts = [
+            pieces_of = [
                 plan.move(acc[j, b * units : (b + 1) * units], shift, plan.shifts[j]) for j in range(3)
             ]
-            own[h, b] = plan.pack(*parts).astype(b16)
-        reduce_start(h)
+            own[h, b] = plan.pack(*pieces_of).astype(b16)
+        for p in range(parts):
+            reduce_start(h, p)
 
     def apply_head(h, slots):
         cut = plan.columns(h)
 
         def body(i, _):
             at_steps(i, slots)
-            span = pl.ds(pl.multiple_of(i * step, step), step)
+            span = pl.ds(pl.multiple_of(i * long, long), long)
             query = keys[span, cut]
-            gate = dot(query, weights[0], 1, 1)
-            up = dot(query, weights[1], 1, 1)
+            gate = dot(weights[0], query, 1, 1)
+            up = dot(weights[1], query, 1, 1)
             mixed = (jax.nn.silu(gate) * up).astype(b16)
-            out = dot(mixed, weights[2], 1, 0)
+            out = dot(mixed, weights[2], 0, 0)
             if h % 2:
                 shared = slice(cut.start, cut.start + 128)
                 outs[span, shared] = outs[span, shared] + out[:, :128]
@@ -642,13 +701,14 @@
                 row[:, span] = jnp.sum(total.T, axis=0, keepdims=True)
             return 0
 
-        lax.fori_loop(0, tokens // step, body, 0)
+        lax.fori_loop(0, tokens // long, body, 0)
 
     def ready(g, h):
         if h % 2 == 0:
             for i in (2,) if g else (0, 1):
                 load(i, h // 2).wait()
-        arrived(g, h)
+        for p in range(parts):
+            arrived(g, h, p)
         (prepare_new if g else prepare_old)(h)
 
     handlers = {
@@ -664,14 +724,14 @@
     order = list(order)
     while order:
         event = order.pop(0)
-        if event == (RELAY, 0, 0, 1):
+        if event == (RELAY, 0, 0, 0, 1):
             turn_rates()
         if event[0] != READY:
             handlers[event[0]](*event[1:])
             continue
         ready(*event[1:])
         slots = {}
-        for k in range(tokens // step):
+        for k in range(tokens // (long if event[1] else step)):
             while order[0][0] != STEP:
                 kind, *rest = order.pop(0)
                 slots.setdefault(k, []).append(functools.partial(handlers[kind], *rest))
@@ -696,12 +756,16 @@
         done()
 
 
-def finish_kernel(step, outs_ref, row_ref, gain_ref, fresh_ref, out_hbm, gate_ref, up_ref, down_ref, staged, sem):
+def finish_kernel(step, outs_ref, row_ref, gain_ref, fresh_ref, out_hbm, *rest):
+    weights, laid, staged, sem, weight_sem = rest[:3], rest[3], rest[4], rest[5], rest[6]
     tokens, width = outs_ref.shape
 
     def store(i):
         span = pl.ds(i * step, step)
         return pltpu.make_async_copy(staged.at[span], out_hbm.at[span], sem.at[i])
+
+    def lay(j):
+        return pltpu.make_async_copy(laid.at[j], weights[j], weight_sem.at[j])
 
     for i in range(tokens // step):
         span = slice(i * step, (i + 1) * step)
@@ -710,11 +774,14 @@
             cut = slice(c, c + 128)
             staged[span, cut] = (outs_ref[span, cut] * scale * gain_ref[cut][None]).astype(staged.dtype)
         store(i).start()
-    for j, ref in enumerate((gate_ref, up_ref, down_ref)):
-        heads = [fresh_ref[j, h].astype(jnp.float32) for h in range(fresh_ref.shape[1])]
-        ref[...] = jnp.stack(heads, axis=1).astype(ref.dtype)
+        if i < len(weights):
+            heads = [fresh_ref[i, h].astype(jnp.float32) for h in range(fresh_ref.shape[1])]
+            laid[i] = jnp.stack(heads, axis=1).astype(laid.dtype)
+            lay(i).start()
     for i in range(tokens // step):
         store(i).wait()
+    for j in range(len(weights)):
+        lay(j).wait()
 
 
 def finish(outs, row, gain, fresh):
@@ -726,10 +793,12 @@
         functools.partial(finish_kernel, step),
         out_shape=(jax.ShapeDtypeStruct(outs.shape, jnp.bfloat16),) + (weight,) * 3,
         in_specs=vmem(4),
-        out_specs=(pl.BlockSpec(memory_space=pl.ANY),) + tuple(vmem(3)),
+        out_specs=(pl.BlockSpec(memory_space=pl.ANY),) * 4,
         scratch_shapes=[
+            pltpu.VMEM((3,) + weight.shape, weight.dtype),
             pltpu.VMEM(outs.shape, jnp.bfloat16),
             pltpu.SemaphoreType.DMA((rows // step,)),
+            pltpu.SemaphoreType.DMA((3,)),
         ],
         compiler_params=pltpu.CompilerParams(vmem_limit_bytes=32 * 1024 * 1024),
         name="finish_rows",
@@ -745,6 +814,7 @@
     hbm = pl.BlockSpec(memory_space=pl.ANY)
     block = (units, plan.packed)
     dma = pltpu.SemaphoreType.DMA
+    copies = 2 * heads
     return pl.pallas_call(
         functools.partial(fused_kernel, plan),
         out_shape=(
@@ -772,16 +842,16 @@
             pltpu.VMEM((1, rows), f32),
             pltpu.VMEM((peers - 1, 1, rows), f32),
             dma((3, heads // 2)),
-            dma((2, heads, 2, outer)),
-            dma((2, heads, outer)),
-            dma((2, heads, outer)),
-            dma((2, heads, outer)),
-            dma((2, heads, 2)),
-            dma((2, heads, 2)),
-            dma((heads, 2, outer)),
-            dma((heads, 2, outer)),
-            dma((heads, outer)),
-            dma((heads, outer)),
+            dma((2, copies, 2, outer)),
+            dma((2, copies, outer)),
+            dma((2, copies, outer)),
+            dma((2, copies, outer)),
+            dma((2, copies, 2)),
+            dma((2, copies, 2)),
+            dma((copies, 2, outer)),
+            dma((copies, 2, outer)),
+            dma((copies, outer)),
+            dma((copies, outer)),
             dma((peers - 1,)),
             dma((peers - 1,)),
         ],

time: 104 us -> 101 us (0.971)
  Pallas kernels: 103 us -> 99.9 us
    pallas_call x1, Pallas kernels: 99.3 us -> 97.2 us  [fused(): pl.pallas_call(functools.partial(fused_kernel, plan), out_shape=(pltpu.VM...]
where the time goes in v4:
time: 101 us
  Pallas kernels  99.9 us (99%)
    pallas_call x1, Pallas kernels, fused(): pl.pallas_call(functools.partial(fused_kernel, plan), out_shape=(pltpu.VM...  97.2 us
    pallas_call x1, Pallas kernels, finish(): pl.pallas_call(functools.partial(finish_kernel, step), out_shape=(jax.Sha...  2.74 us

profile of v4, /device:TPU:0, one launch (start us, length us, event | category | flops | bytes accessed | tf_op | source)
XLA Modules:
  0.0 100.8 jit_solution(7537028188181569890)
XLA Ops:
  0.6 0.0 copy-start
  0.6 97.2 %fused_layer.1 = (f32[2048,1280]{1,0:T(8,128)S(1)}, f32[1,2048]{1,0:T(1,128)S(1)}, bf16[3,4,40,320]{3,2,1,0:T(8,128)(2,1)S(1)}) custom-call(bf16[2048,1280]{1,0:T(8,128)(2,1)} %key_hbm.1, bf16[2048,1280]{1,0:T(8,128)(2,1)} %value_hbm.1, bf16[2048,1280]{1,0:T(8,128)(2,1)} %query_hbm.1, f32[4,2048]{1,0:T(4,128)} %bitcast.1, bf16[40,4,320]{2,1,0:T(4,128)(2,1)} %gate_ref.1, ...), custom_call_target="tpu_custom_call" | custom-call | tf_op jit(solution)/shard_map/fused_layer/pallas_call | solution.py:818
  97.8 0.0 copy-done
  97.8 2.7 %finish_rows.1 = (bf16[2048,1280]{1,0:T(8,128)(2,1)}, bf16[40,4,320]{2,1,0:T(4,128)(2,1)}, bf16[40,4,320]{2,1,0:T(4,128)(2,1)}, bf16[40,4,320]{2,1,0:T(4,128)(2,1)}) custom-call(f32[2048,1280]{1,0:T(8,128)S(1)} %get-tuple-element.7.outs_ref, f32[1,2048]{1,0:T(1,128)S(1)} %get-tuple-element.8.row_ref, f32[1280]{0:T(1024)S(1)} %copy-done, ...), custom_call_target="tpu_custom_call" | custom-call | tf_op jit(solution)/shard_map/finish_rows/pallas_call | solution.py:792
Async XLA Ops:
  0.6 97.2 %copy-start = (f32[1280]{0:T(1024)S(1)}, f32[1280]{0:T(1024)}, u32[]{:S(2)}) copy-start(f32[1280]{0:T(1024)} %gain_ref.1) | copy-start | bytes 15364

commit v5 on v4

--- a/solution.py
+++ b/solution.py
@@ -11,7 +11,7 @@
 EPS = 1e-06
 
 VMEM_LIMIT = 50 * 1024 * 1024
-STEPS = (1024, 1024)
+STEPS = (1024, 2048)
 ISSUE, RELAY, CROSS, READY, STEP, START, SIDE, PART, END, FINISH = range(10)
 ORDERS = {
     (4, 4, 2048): (
@@ -19,41 +19,39 @@
         (((0, 1), (0, 1), (0, 1), (0, 1)), ((0, 1), (0, 1), (0, 1), (2, 2))),
         (
             (ISSUE, 0, 0, 0), (ISSUE, 0, 0, 1), (ISSUE, 0, 1, 0), (ISSUE, 0, 1, 1),
-            (RELAY, 0, 0, 0, 1), (RELAY, 0, 0, 1, 1), (RELAY, 0, 1, 0, 1), (CROSS, 0, 0, 1),
+            (RELAY, 0, 0, 0, 1), (RELAY, 0, 0, 1, 1), (CROSS, 0, 0, 1), (RELAY, 0, 1, 0, 1),
             (RELAY, 0, 0, 0, 2), (RELAY, 0, 0, 1, 2), (RELAY, 0, 1, 1, 1), (ISSUE, 0, 2, 0),
             (ISSUE, 0, 2, 1), (CROSS, 0, 1, 1), (RELAY, 0, 0, 0, 3), (RELAY, 0, 0, 1, 3),
             (RELAY, 0, 1, 1, 2), (RELAY, 0, 1, 0, 2), (ISSUE, 0, 3, 0), (ISSUE, 0, 3, 1),
             (READY, 0, 0), (RELAY, 0, 2, 0, 1), (STEP, 0, 0, 0), (RELAY, 0, 1, 1, 3),
             (RELAY, 0, 1, 0, 3), (RELAY, 0, 2, 1, 1), (CROSS, 0, 2, 1), (STEP, 0, 0, 1),
-            (CROSS, 0, 3, 1), (START, 0), (RELAY, 0, 2, 0, 2), (RELAY, 0, 2, 1, 2),
-            (RELAY, 0, 3, 0, 1), (READY, 0, 1), (STEP, 0, 1, 0), (RELAY, 0, 2, 0, 3),
-            (RELAY, 0, 2, 1, 3), (STEP, 0, 1, 1), (RELAY, 0, 3, 0, 2), (RELAY, 0, 3, 0, 3),
+            (CROSS, 0, 3, 1), (START, 0), (RELAY, 0, 2, 1, 2), (RELAY, 0, 2, 0, 2),
+            (RELAY, 0, 3, 0, 1), (READY, 0, 1), (STEP, 0, 1, 0), (RELAY, 0, 2, 1, 3),
+            (RELAY, 0, 2, 0, 3), (STEP, 0, 1, 1), (RELAY, 0, 3, 0, 2), (RELAY, 0, 3, 0, 3),
             (RELAY, 0, 3, 1, 1), (START, 1), (READY, 0, 2), (STEP, 0, 2, 0), (RELAY, 0, 3, 1, 2),
             (RELAY, 0, 3, 1, 3), (PART, 0, 0, 3, 1), (PART, 0, 0, 2, 1), (STEP, 0, 2, 1),
-            (START, 2), (SIDE, 1, 1, 1), (PART, 0, 1, 3, 1), (SIDE, 1, 1, 2), (SIDE, 1, 1, 3),
-            (PART, 0, 0, 3, 2), (SIDE, 1, 1, 0), (PART, 0, 1, 2, 1), (READY, 0, 3),
-            (STEP, 0, 3, 0), (PART, 0, 1, 3, 2), (SIDE, 2, 0, 3), (END, 0, 0), (SIDE, 2, 0, 2),
-            (SIDE, 2, 0, 0), (END, 0, 1), (SIDE, 2, 0, 1), (PART, 1, 0, 3, 1), (PART, 1, 0, 2, 1),
-            (STEP, 0, 3, 1), (START, 3), (PART, 1, 1, 3, 1), (FINISH, 0, 0), (FINISH, 0, 1),
-            (SIDE, 2, 1, 2), (PART, 1, 1, 2, 1), (SIDE, 2, 1, 0), (PART, 1, 0, 3, 2),
-            (PART, 2, 0, 3, 1), (PART, 2, 0, 2, 1), (SIDE, 2, 1, 3), (SIDE, 2, 1, 1),
-            (PART, 1, 1, 3, 2), (END, 1, 0), (RELAY, 1, 0, 0, 1), (RELAY, 1, 0, 1, 1),
-            (SIDE, 3, 0, 3), (END, 1, 1), (FINISH, 1, 1), (SIDE, 3, 0, 0), (PART, 2, 0, 3, 2),
-            (SIDE, 3, 1, 0), (SIDE, 3, 0, 1), (SIDE, 3, 1, 3), (RELAY, 1, 0, 0, 2),
-            (RELAY, 1, 0, 0, 3), (PART, 2, 1, 3, 1), (SIDE, 3, 0, 2), (PART, 2, 1, 2, 1),
-            (RELAY, 1, 0, 1, 2), (END, 2, 0), (FINISH, 2, 0), (SIDE, 3, 1, 2), (RELAY, 1, 1, 1, 1),
-            (FINISH, 1, 0), (RELAY, 1, 0, 1, 3), (PART, 3, 0, 3, 1), (PART, 2, 1, 3, 2),
-            (END, 2, 1), (FINISH, 2, 1), (RELAY, 1, 1, 1, 2), (PART, 3, 1, 3, 1),
-            (RELAY, 1, 2, 0, 1), (PART, 3, 0, 3, 2), (PART, 3, 0, 2, 1), (RELAY, 1, 1, 0, 1),
-            (SIDE, 3, 1, 1), (PART, 3, 1, 3, 2), (CROSS, 1, 0, 1), (RELAY, 1, 2, 1, 1),
-            (PART, 3, 1, 2, 1), (RELAY, 1, 2, 0, 2), (END, 3, 0), (RELAY, 1, 1, 0, 2),
-            (FINISH, 3, 0), (RELAY, 1, 2, 1, 2), (RELAY, 1, 1, 0, 3), (RELAY, 1, 1, 1, 3),
-            (CROSS, 1, 1, 1), (END, 3, 1), (FINISH, 3, 1), (READY, 1, 0), (STEP, 1, 0, 0),
-            (RELAY, 1, 2, 0, 3), (RELAY, 1, 3, 0, 1), (RELAY, 1, 3, 0, 2), (CROSS, 1, 2, 1),
-            (RELAY, 1, 2, 1, 3), (STEP, 1, 0, 1), (READY, 1, 1), (RELAY, 1, 3, 0, 3),
-            (STEP, 1, 1, 0), (RELAY, 1, 3, 1, 1), (RELAY, 1, 3, 1, 2), (RELAY, 1, 3, 1, 3),
-            (STEP, 1, 1, 1), (READY, 1, 2), (STEP, 1, 2, 0), (STEP, 1, 2, 1), (READY, 1, 3),
-            (STEP, 1, 3, 0), (STEP, 1, 3, 1),
+            (START, 2), (PART, 0, 1, 3, 1), (SIDE, 1, 1, 0), (SIDE, 1, 1, 2), (SIDE, 1, 1, 1),
+            (PART, 0, 0, 3, 2), (SIDE, 1, 1, 3), (PART, 0, 1, 2, 1), (READY, 0, 3),
+            (STEP, 0, 3, 0), (PART, 0, 1, 3, 2), (SIDE, 2, 0, 3), (END, 0, 0), (SIDE, 2, 0, 1),
+            (SIDE, 2, 0, 2), (PART, 1, 0, 3, 1), (SIDE, 2, 0, 0), (PART, 1, 0, 2, 1), (END, 0, 1),
+            (STEP, 0, 3, 1), (START, 3), (PART, 1, 1, 3, 1), (FINISH, 0, 0), (PART, 1, 1, 2, 1),
+            (SIDE, 2, 1, 3), (FINISH, 0, 1), (SIDE, 2, 1, 0), (PART, 1, 0, 3, 2),
+            (PART, 2, 0, 3, 1), (PART, 2, 0, 2, 1), (SIDE, 3, 0, 3), (SIDE, 2, 1, 2),
+            (PART, 1, 1, 3, 2), (SIDE, 2, 1, 1), (END, 1, 0), (RELAY, 1, 0, 0, 1), (SIDE, 3, 0, 0),
+            (END, 1, 1), (FINISH, 1, 1), (SIDE, 3, 0, 2), (RELAY, 1, 0, 1, 1), (SIDE, 3, 1, 3),
+            (PART, 2, 0, 3, 2), (SIDE, 3, 0, 1), (END, 2, 0), (FINISH, 2, 0), (PART, 2, 1, 3, 1),
+            (PART, 2, 1, 2, 1), (SIDE, 3, 1, 0), (RELAY, 1, 0, 0, 2), (RELAY, 1, 0, 0, 3),
+            (SIDE, 3, 1, 1), (RELAY, 1, 0, 1, 2), (RELAY, 1, 0, 1, 3), (PART, 3, 0, 3, 1),
+            (RELAY, 1, 1, 1, 1), (FINISH, 1, 0), (PART, 2, 1, 3, 2), (SIDE, 3, 1, 2),
+            (CROSS, 1, 0, 1), (END, 2, 1), (FINISH, 2, 1), (PART, 3, 1, 3, 1), (RELAY, 1, 1, 1, 2),
+            (PART, 3, 0, 3, 2), (RELAY, 1, 1, 1, 3), (RELAY, 1, 1, 0, 1), (RELAY, 1, 2, 0, 1),
+            (PART, 3, 0, 2, 1), (READY, 1, 0), (PART, 3, 1, 3, 2), (RELAY, 1, 2, 1, 1),
+            (RELAY, 1, 1, 0, 2), (PART, 3, 1, 2, 1), (CROSS, 1, 1, 1), (RELAY, 1, 2, 0, 2),
+            (END, 3, 0), (FINISH, 3, 0), (RELAY, 1, 1, 0, 3), (RELAY, 1, 2, 1, 2), (END, 3, 1),
+            (FINISH, 3, 1), (STEP, 1, 0, 0), (RELAY, 1, 2, 0, 3), (READY, 1, 1),
+            (RELAY, 1, 3, 0, 1), (RELAY, 1, 3, 0, 2), (CROSS, 1, 2, 1), (RELAY, 1, 2, 1, 3),
+            (RELAY, 1, 3, 0, 3), (RELAY, 1, 3, 1, 1), (RELAY, 1, 3, 1, 2), (RELAY, 1, 3, 1, 3),
+            (STEP, 1, 1, 0), (READY, 1, 2), (STEP, 1, 2, 0), (READY, 1, 3), (STEP, 1, 3, 0),
         ),
     ),
 }

time: 101 us -> 98.9 us (0.979)
  Pallas kernels: 99.9 us -> 97.9 us
    pallas_call x1, Pallas kernels: 97.2 us -> 95.1 us  [fused(): pl.pallas_call(functools.partial(fused_kernel, plan), out_shape=(pltpu.VM...]
where the time goes in v5:
time: 98.9 us; the launch traced here: 98.7 us
  Pallas kernels  97.9 us (99%)
    pallas_call x1, Pallas kernels, fused(): pl.pallas_call(functools.partial(fused_kernel, plan), out_shape=(pltpu.VM...  95.1 us
    pallas_call x1, Pallas kernels, finish(): pl.pallas_call(functools.partial(finish_kernel, step), out_shape=(jax.Sha...  2.74 us

profile of v5, /device:TPU:0, one launch (start us, length us, event | category | flops | bytes accessed | tf_op | source)
XLA Modules:
  0.0 98.7 jit_solution(2187488418904832506)
XLA Ops:
  0.6 0.0 copy-start
  0.6 95.1 %fused_layer.1 = (f32[2048,1280]{1,0:T(8,128)S(1)}, f32[1,2048]{1,0:T(1,128)S(1)}, bf16[3,4,40,320]{3,2,1,0:T(8,128)(2,1)S(1)}) custom-call(bf16[2048,1280]{1,0:T(8,128)(2,1)} %key_hbm.1, bf16[2048,1280]{1,0:T(8,128)(2,1)} %value_hbm.1, bf16[2048,1280]{1,0:T(8,128)(2,1)} %query_hbm.1, f32[4,2048]{1,0:T(4,128)} %bitcast.1, bf16[40,4,320]{2,1,0:T(4,128)(2,1)} %gate_ref.1, ...), custom_call_target="tpu_custom_call" | custom-call | tf_op jit(solution)/shard_map/fused_layer/pallas_call | solution.py:816
  95.8 0.0 copy-done
  95.8 2.7 %finish_rows.1 = (bf16[2048,1280]{1,0:T(8,128)(2,1)}, bf16[40,4,320]{2,1,0:T(4,128)(2,1)}, bf16[40,4,320]{2,1,0:T(4,128)(2,1)}, bf16[40,4,320]{2,1,0:T(4,128)(2,1)}) custom-call(f32[2048,1280]{1,0:T(8,128)S(1)} %get-tuple-element.7.outs_ref, f32[1,2048]{1,0:T(1,128)S(1)} %get-tuple-element.8.row_ref, f32[1280]{0:T(1024)S(1)} %copy-done, ...), custom_call_target="tpu_custom_call" | custom-call | tf_op jit(solution)/shard_map/finish_rows/pallas_call | solution.py:790
Async XLA Ops:
  0.6 95.2 %copy-start = (f32[1280]{0:T(1024)S(1)}, f32[1280]{0:T(1024)}, u32[]{:S(2)}) copy-start(f32[1280]{0:T(1024)} %gain_ref.1) | copy-start | bytes 15364

commit v6 on v5

--- a/solution.py
+++ b/solution.py
@@ -786,7 +786,7 @@
     rows, width = outs.shape
     units, heads = fresh.shape[2], fresh.shape[1]
     weight = jax.ShapeDtypeStruct((units, heads, fresh.shape[3]), fresh.dtype)
-    step = 256
+    step = math.gcd(rows, 128)
     return pl.pallas_call(
         functools.partial(finish_kernel, step),
         out_shape=(jax.ShapeDtypeStruct(outs.shape, jnp.bfloat16),) + (weight,) * 3,

time: 98.9 us -> 99.1 us (level)
  no operation moved by 1% of the time
where the time goes in v6:
time: 99.1 us; the launch traced here: 98.9 us
  Pallas kernels  98.1 us (99%)
    pallas_call x1, Pallas kernels, fused(): pl.pallas_call(functools.partial(fused_kernel, plan), out_shape=(pltpu.VM...  95.1 us
    pallas_call x1, Pallas kernels, finish(): pl.pallas_call(functools.partial(finish_kernel, step), out_shape=(jax.Sha...  2.93 us

profile of v6, /device:TPU:0, one launch (start us, length us, event | category | flops | bytes accessed | tf_op | source)
XLA Modules:
  0.0 98.9 jit_solution(11186868173842849956)
XLA Ops:
  0.6 0.0 copy-start
  0.6 95.1 %fused_layer.1 = (f32[2048,1280]{1,0:T(8,128)S(1)}, f32[1,2048]{1,0:T(1,128)S(1)}, bf16[3,4,40,320]{3,2,1,0:T(8,128)(2,1)S(1)}) custom-call(bf16[2048,1280]{1,0:T(8,128)(2,1)} %key_hbm.1, bf16[2048,1280]{1,0:T(8,128)(2,1)} %value_hbm.1, bf16[2048,1280]{1,0:T(8,128)(2,1)} %query_hbm.1, f32[4,2048]{1,0:T(4,128)} %bitcast.1, bf16[40,4,320]{2,1,0:T(4,128)(2,1)} %gate_ref.1, ...), custom_call_target="tpu_custom_call" | custom-call | tf_op jit(solution)/shard_map/fused_layer/pallas_call | solution.py:816
  95.8 0.0 copy-done
  95.8 2.9 %finish_rows.1 = (bf16[2048,1280]{1,0:T(8,128)(2,1)}, bf16[40,4,320]{2,1,0:T(4,128)(2,1)}, bf16[40,4,320]{2,1,0:T(4,128)(2,1)}, bf16[40,4,320]{2,1,0:T(4,128)(2,1)}) custom-call(f32[2048,1280]{1,0:T(8,128)S(1)} %get-tuple-element.7.outs_ref, f32[1,2048]{1,0:T(1,128)S(1)} %get-tuple-element.8.row_ref, f32[1280]{0:T(1024)S(1)} %copy-done, ...), custom_call_target="tpu_custom_call" | custom-call | tf_op jit(solution)/shard_map/finish_rows/pallas_call | solution.py:790
Async XLA Ops:
  0.6 95.2 %copy-start = (f32[1280]{0:T(1024)S(1)}, f32[1280]{0:T(1024)}, u32[]{:S(2)}) copy-start(f32[1280]{0:T(1024)} %gain_ref.1) | copy-start | bytes 15364
